TPU v7x, 32 devices: a whole 2x2x4 slice. The times are simulated.
32 devices in a mesh: table: 16 (over z, y, x), tensor: 2 (over core).
Axes of the slice: x: 2, y: 2, z: 4, core: 2. Of those that a mesh axis runs over, the one named last changes fastest.
Arguments:
- hidden: bfloat16 [512, 2560], P('table'), may hold values from -16 to 16
- attn_gain: float32 [2560], replicated, may hold values from 0.6 to 1.4
- q_weight: bfloat16 [2560, 2560], P(None, 'tensor'), may hold values from -1 to 1
- kv_weight: bfloat16 [2560, 2, 512], P(None, None, 'tensor'), may hold values from -0.125 to 0.125
- out_weight: bfloat16 [2560, 2560], P('tensor'), may hold values from -0.125 to 0.125
- key_cache: bfloat16 [512, 256, 512], P('table', None, 'tensor'), may hold values from -256 to 256
- value_cache: bfloat16 [512, 256, 512], P('table', None, 'tensor'), may hold values from -6 to 6
- cache_lengths: int32 [512], P('table'), may hold values from 64 to 256
- table: bfloat16 [65536, 1280], P('table'), may hold values from -6 to 6
- key_proj: bfloat16 [1280, 2560], P(None, 'tensor'), may hold values from -0.15625 to 0.15625
- value_proj: bfloat16 [1280, 2560], P(None, 'tensor'), may hold values from -0.15625 to 0.15625
- lookup_ids: int32 [512, 16], P('table'), may hold values from 0 to 65535, as said below
Outputs:
- mixed: bfloat16 [512, 2560], P('table', 'tensor')
Inputs may be any that keep to these rules, and one draw needn't show every extreme that they name: `lookup_ids`: within the 32 sequences of one index of table (aligned blocks of rows), at most 64 ids lie in the range of 4096 rows of any one owner (owner = id // 4096); in every draw one owner gets exactly 64 ids from every block.
All inputs are finite; a program needn't handle non-finite values.
Results may differ from a plain program's by a relative error of at most 0.007.
Values may be sent and summed in bfloat16 or wider, within the bound.
A program may use at most 128 MiB of HBM per device.

v0:
```python
import math

import jax
import jax.numpy as jnp
from jax import lax
from jax.sharding import PartitionSpec as P

HEAD_DIM = 128


epsilon = 1e-06


def local(
    hidden,
    attn_gain,
    q_weight,
    kv_weight,
    out_weight,
    key_cache,
    value_cache,
    cache_lengths,
    table,
    key_proj,
    value_proj,
    lookup_ids,
):
    seq_count, width = hidden.shape
    tensor_count = lax.axis_size("tensor")
    tensor_index = lax.axis_index("tensor")
    slice_width = width // tensor_count
    hidden_f32 = hidden.astype(jnp.float32)
    normed = hidden_f32 * lax.rsqrt(
        jnp.mean(hidden_f32 * hidden_f32, axis=1, keepdims=True) + epsilon
    )
    attn_in = (normed * attn_gain).astype(jnp.bfloat16)
    head_dim = HEAD_DIM
    ctx_len = key_cache.shape[1]
    kv_width = kv_weight.shape[2]
    kv_local = kv_width // head_dim
    group_size = q_weight.shape[1] // kv_width
    inv_scale = 1.0 / math.sqrt(head_dim)
    query_proj = jnp.dot(attn_in, q_weight, preferred_element_type=jnp.float32).astype(jnp.bfloat16)
    new_kv = jnp.dot(
        attn_in, kv_weight.reshape(width, 2 * kv_width), preferred_element_type=jnp.float32
    ).astype(jnp.bfloat16)
    query_heads = query_proj.reshape(seq_count, kv_local, group_size, head_dim)
    new_key = new_kv[:, :kv_width].reshape(seq_count, kv_local, head_dim)
    new_value = new_kv[:, kv_width:].reshape(seq_count, kv_local, head_dim)
    key_blocks = key_cache.reshape(seq_count, ctx_len, kv_local, head_dim)
    value_blocks = value_cache.reshape(seq_count, ctx_len, kv_local, head_dim)
    attention_energies = (
        jnp.einsum("skgh,sckh->skgc", query_heads, key_blocks, preferred_element_type=jnp.float32)
        * inv_scale
    )
    own_score = (
        jnp.einsum("skgh,skh->skg", query_heads, new_key, preferred_element_type=jnp.float32)
        * inv_scale
    )
    valid_mask = jnp.arange(ctx_len, dtype=jnp.int32)[None, :] < cache_lengths[:, None]
    masked = jnp.where(valid_mask[:, None, None, :], attention_energies, -1e30)
    row_max = jnp.maximum(jnp.max(masked, axis=-1), own_score)
    weights = jnp.exp(masked - row_max[..., None])
    own_weight = jnp.exp(own_score - row_max)
    denom_sum = jnp.sum(weights, axis=-1) + own_weight
    weights_bf = (weights / denom_sum[..., None]).astype(jnp.bfloat16)
    own_prob = (own_weight / denom_sum).astype(jnp.bfloat16)
    context = jnp.einsum(
        "skgc,sckh->skgh", weights_bf, value_blocks, preferred_element_type=jnp.float32
    )
    context = (
        context
        + own_prob.astype(jnp.float32)[..., None] * new_value.astype(jnp.float32)[:, :, None, :]
    )
    context = context.reshape(seq_count, -1).astype(jnp.bfloat16)
    attention = jnp.dot(context, out_weight, preferred_element_type=jnp.float32)
    rows_dev, emb_width = table.shape
    table_count = lax.axis_size("table")
    flat_ids = lookup_ids.reshape(-1)
    requests = flat_ids.shape[0]
    capacity = max(2, 2 * requests // table_count)
    owner_of = flat_ids // rows_dev
    local_row = flat_ids - owner_of * rows_dev
    positions = jnp.arange(requests, dtype=jnp.int32)
    earlier = (owner_of[None, :] == owner_of[:, None]) & (positions[None, :] < positions[:, None])
    rank_of = jnp.sum(earlier.astype(jnp.int32), axis=1)
    slot_of = owner_of * capacity + rank_of
    outgoing = jnp.full((table_count * capacity,), -1, jnp.int32).at[slot_of].set(local_row)
    outgoing = outgoing.reshape(table_count, capacity)
    part_width = emb_width // tensor_count
    wanted = jnp.take(
        table,
        jnp.maximum(lax.all_to_all(outgoing, "table", split_axis=0, concat_axis=0, tiled=True), 0),
        axis=0,
    )
    wanted = lax.dynamic_slice_in_dim(wanted, tensor_index * part_width, part_width, 2)
    replies = lax.all_to_all(wanted, "table", split_axis=0, concat_axis=0, tiled=True)
    mem_rows = jnp.take(replies.reshape(table_count * capacity, replies.shape[2]), slot_of, axis=0)
    mem_rows = lax.all_gather(mem_rows, "tensor", axis=1, tiled=True)
    lookups = lookup_ids.shape[1]
    mem_key = jnp.dot(mem_rows, key_proj, preferred_element_type=jnp.float32).reshape(
        seq_count, lookups, slice_width
    )
    mem_value = jnp.dot(mem_rows, value_proj, preferred_element_type=jnp.float32).reshape(
        seq_count, lookups, slice_width
    )
    normed_slice = lax.dynamic_slice_in_dim(normed, tensor_index * slice_width, slice_width, 1)
    cross_term = jnp.sum(mem_key * normed_slice[:, None, :], axis=-1)
    square_sum = jnp.sum(mem_key * mem_key, axis=-1)
    cross_term, square_sum = lax.psum((cross_term, square_sum), "tensor")
    gating = jax.nn.sigmoid(cross_term * lax.rsqrt(square_sum / width + epsilon) / math.sqrt(width))
    memory = jnp.sum(gating[..., None] * mem_value, axis=1)
    attention_part = lax.psum_scatter(
        attention.astype(jnp.bfloat16), "tensor", scatter_dimension=1, tiled=True
    ).astype(jnp.float32)
    residual = lax.dynamic_slice_in_dim(hidden_f32, tensor_index * slice_width, slice_width, 1)
    return (residual + attention_part + memory).astype(jnp.bfloat16)


def solution(mesh):
    return jax.shard_map(
        local,
        mesh=mesh,
        in_specs=(
            P("table", None),
            P(),
            P(None, "tensor"),
            P(None, None, "tensor"),
            P("tensor", None),
            P("table", None, "tensor"),
            P("table", None, "tensor"),
            P("table"),
            P("table", None),
            P(None, "tensor"),
            P(None, "tensor"),
            P("table", None),
        ),
        out_specs=P("table", "tensor"),
        check_vma=False,
    )
```

profile of v0, /device:TPU:0, one launch (start us, length us, event | category | flops | bytes accessed | tf_op | source)
XLA Modules:
  0.0 115.9 jit_solution(4010920063350452005)
XLA Ops:
  6.5 0.9 copy.30
  7.9 2.4 %scatter_custom_fusion = s32[1024]{0:T(1024)S(1)} fusion(s32[512]{0:T(512)S(1)} %bitcast.62, s32[512]{0:T(512)S(1)} %get-tuple-element.9, s32[]{:T(128)} %constant.78.clone.1), kind=kCustom, calls=%fused_computation.57 | custom fusion | bytes 4100 | tf_op jit(solution)/shard_map/scatter | solution.py:88
  11.0 8.3 %all-to-all-start = ((s32[16,1,64]{2,1,0:T(1,128)}), s32[16,1,64]{2,1,0:T(1,128)S(1)}, u32[]{:S(2)}, u32[]{:S(2)}) async-start(s32[16,1,64]{2,1,0:T(1,128)} %all_to_all.9), calls=%async_computation.1 | async-start | bytes 16384 | tf_op jit(solution)/shard_map/all_to_all | solution.py:93
  19.4 7.2 %all-to-all-done = s32[16,1,64]{2,1,0:T(1,128)S(1)} async-done(((s32[16,1,64]{2,1,0:T(1,128)}), s32[16,1,64]{2,1,0:T(1,128)S(1)}, u32[]{:S(2)}, u32[]{:S(2)}) %all-to-all-start) | async-done | bytes 4128 | tf_op jit(solution)/shard_map/all_to_all | solution.py:93
  26.7 11.9 %gather_fusion = bf16[1024,1280]{1,0:T(8,128)(2,1)} fusion(bf16[4096,1280]{1,0:T(8,128)(2,1)} %param.20, s32[1024]{0:T(1024)S(1)} %broadcast_clamp_fusion), kind=kCustom, calls=%fused_computation | custom fusion | bytes 5246976 | tf_op jit(solution)/shard_map/jit(_take)/gather | solution.py:91
  38.6 2.7 %dynamic-slice_select_fusion = bf16[16,64,640]{2,1,0:T(8,128)(2,1)} fusion(bf16[16,64,1280]{2,1,0:T(8,128)(2,1)} %bitcast.55, s32[]{:T(128)S(6)} %select_n.68, pred[16,64]{1,0:T(8,128)(4,1)S(1)} %compare_bitcast_fusion), kind=kLoop, calls=%fused_computation.15 | loop fusion | flops 655360 | bytes 2622468 | tf_op jit(solution)/shard_map/jit(_take)/select_n | solution.py:91
  41.3 4.4 %all-to-all-start.1 = ((bf16[16,64,640]{2,1,0:T(8,128)(2,1)}), bf16[16,64,640]{2,1,0:T(8,128)(2,1)}, u32[]{:S(2)}, u32[]{:S(2)}) async-start(bf16[16,64,640]{2,1,0:T(8,128)(2,1)} %dynamic-slice_select_fusion), calls=%async_computation.2 | async-start | bytes 2621440 | tf_op jit(solution)/shard_map/all_to_all | solution.py:97
  45.8 2.2 %copy.37 = bf16[320,8,2,256]{3,1,2,0:T(8,128)(2,1)S(1)} copy(bf16[320,8,2,256]{3,2,1,0:T(2,128)(2,1)} %bitcast.56) | data formatting | bytes 5242880
  50.0 4.1 %convolution_convert_fusion.1 = bf16[32,1280]{1,0:T(8,128)(2,1)S(1)} fusion(bf16[2560,1280]{1,0:T(8,128)(2,1)} %param.14, f32[2560]{0:T(1024)S(1)} %copy-done.2, f32[32]{0:T(128)S(1)} %add_rsqrt_fusion, bf16[32,2560]{1,0:T(8,128)(2,1)S(1)} %copy-done.1), kind=kOutput, calls=%fused_computation.14 | convolution fusion | flops 210083840 | bytes 6809728 | tf_op jit(solution)/shard_map/dot_general | solution.py:43
  55.1 1.1 fusion.30
  56.2 4.3 %fusion.29 = (f32[32,2,5]{2,1,0:T(2,128)S(1)}, f32[32,2,5,256]{3,2,1,0:T(8,128)}) fusion(bf16[32,2,5,128]{3,2,1,0:T(8,128)(2,1)} %reshape.230, pred[32,256]{1,0:T(8,128)(4,1)S(1)} %iota_compare_fusion.1, bf16[32,256,256]{2,1,0:T(8,128)(2,1)} %param.17), kind=kOutput, calls=%fused_computation.65 | convolution fusion | flops 21216960 | bytes 4613376 | tf_op jit(solution)/shard_map/skgh,sckh->skgc/dot_general | solution.py:53
  60.5 13.5 %all-to-all-done.1 = bf16[16,64,640]{2,1,0:T(8,128)(2,1)} async-done(((bf16[16,64,640]{2,1,0:T(8,128)(2,1)}), bf16[16,64,640]{2,1,0:T(8,128)(2,1)}, u32[]{:S(2)}, u32[]{:S(2)}) %all-to-all-start.1) | async-done | bytes 1310752 | tf_op jit(solution)/shard_map/all_to_all | solution.py:97
  74.0 4.3 %gather_fusion.1 = bf16[512,640]{1,0:T(8,128)(2,1)} fusion(bf16[1024,640]{1,0:T(8,128)(2,1)} %bitcast.7, s32[1024]{0:T(1024)S(1)} %pad_clamp_fusion), kind=kCustom, calls=%fused_computation.1 | custom fusion | bytes 1312768 | tf_op jit(solution)/shard_map/jit(_take)/gather | solution.py:98
  78.3 2.1 %broadcast_select_fusion = bf16[512,640]{1,0:T(8,128)(2,1)} fusion(bf16[512,640]{1,0:T(8,128)(2,1)} %gather_fusion.1, pred[512]{0:T(512)(128)(4,1)S(1)} %compare_and_fusion), kind=kLoop, calls=%fused_computation.24 | loop fusion | flops 327680 | bytes 1311232 | tf_op jit(solution)/shard_map/jit(_take)/select_n | solution.py:98
  80.5 1.4 %reshape.239 = f32[32,2,128]{2,1,0:T(2,128)} reshape(f32[32,256]{1,0:T(8,128)} %get-tuple-element.13) | data formatting | bytes 65536 | tf_op jit(solution)/shard_map/convert_element_type | solution.py:73
  81.9 1.3 %fusion.20 = f32[32,2,5]{2,1,0:T(2,128)S(1)} fusion(f32[32,2,5,256]{3,2,1,0:T(8,128)} %get-tuple-element.16, f32[32,2,5]{2,1,0:T(2,128)S(1)} %multiply_maximum_fusion), kind=kLoop, calls=%fused_computation.27 | loop fusion | flops 163520 | bytes 330240 | tf_op jit(solution)/shard_map/reduce_sum | solution.py:65
  83.3 3.7 %fusion.16 = bf16[32,2,5,128]{3,2,1,0:T(8,128)(2,1)} fusion(f32[32,2,5,256]{3,2,1,0:T(8,128)} %get-tuple-element.16, f32[32,2,5]{2,1,0:T(2,128)S(1)} %get-tuple-element.12, f32[32,2,5]{2,1,0:T(2,128)S(1)} %multiply_maximum_fusion, f32[32,2,128]{2,1,0:T(2,128)} %reshape.239, f32[32,2,5]{2,1,0:T(2,128)S(1)} %get-tuple-element.11, bf16[32,256,256]{2,1,0:T(8,128)(2,1)} %param.18), kind=kOutput, calls=%fused_computation.19 | convolution fusion | flops 21340160 | bytes 4640512 | tf_op jit(solution)/shard_map/skgc,sckh->skgh/dot_general | solution.py:68
  87.0 1.0 convert_element_type.59
  88.0 5.0 %convolution_convert_fusion = bf16[32,2560]{1,0:T(8,128)(2,1)} fusion(bf16[32,1280]{1,0:T(8,128)(2,1)S(1)} %convert_element_type.59, bf16[1280,2560]{1,0:T(8,128)(2,1)} %param.16), kind=kOutput, calls=%fused_computation.9 | convolution fusion | flops 209797120 | bytes 6799360 | tf_op jit(solution)/shard_map/dot_general | solution.py:76
  93.9 1.6 %constant_dynamic-slice_fusion = f32[32,1280]{1,0:T(8,128)} fusion(f32[32,2560]{1,0:T(8,128)} %broadcast_multiply_fusion, s32[]{:T(128)S(6)} %select_n.61), kind=kLoop, calls=%fused_computation.62 | loop fusion | bytes 327684 | tf_op jit(solution)/shard_map/dynamic_slice | solution.py:107
  96.2 4.3 %multiply_reduce_fusion.1 = (f32[512]{0:T(512)S(1)}, f32[512]{0:T(512)S(1)}) fusion(f32[32,1280]{1,0:T(8,128)} %constant_dynamic-slice_fusion, bf16[512,1280]{1,0:T(8,128)(2,1)} %all-gather.2.cloned.1.call-done, bf16[1280,1280]{1,0:T(8,128)(2,1)} %param.21), kind=kOutput, calls=%fused_computation.13 | convolution fusion | flops 1680342016 | bytes 4755456 | tf_op jit(solution)/shard_map/dot_general | solution.py:101
  100.7 3.4 %all-reduce = (f32[32,16]{1,0:T(8,128)S(1)}, f32[32,16]{1,0:T(8,128)S(1)}) all-reduce(f32[32,16]{1,0:T(8,128)S(1)} %reduce_sum.65, f32[32,16]{1,0:T(8,128)S(1)} %reduce_sum.67), channel_id=1, replica_groups=mesh['table'=16,'tensor'=2] {'tensor'}, use_global_device_ids=true, to_apply=%region_7.8 | all-reduce | flops 1024 | bytes 8192 | tf_op jit(solution)/shard_map/psum | solution.py:110
  104.1 3.2 %multiply_reduce_fusion = f32[32,1280]{1,0:T(8,128)S(1)} fusion(f32[32,16]{1,0:T(8,128)S(1)} %add_divide_fusion, bf16[512,1280]{1,0:T(8,128)(2,1)} %all-gather.2.cloned.1.call-done, bf16[1280,1280]{1,0:T(8,128)(2,1)S(1)} %copy-done), kind=kOutput, calls=%fused_computation.12 | convolution fusion | flops 1678991360 | bytes 4753408 | tf_op jit(solution)/shard_map/dot_general | solution.py:104
  107.4 1.6 %add_convert_fusion = bf16[32,1280]{1,0:T(8,128)(2,1)} fusion(f32[32,1280]{1,0:T(8,128)S(1)} %multiply_reduce_fusion, bf16[32,1280]{1,0:T(8,128)(2,1)} %reduce-scatter.2.cloned.1.call-done, f32[32,2560]{1,0:T(8,128)} %convert_element_type.49, s32[]{:T(128)S(6)} %select_n.61), kind=kLoop, calls=%fused_computation.32 | loop fusion | flops 163840 | bytes 491524 | tf_op jit(solution)/shard_map/convert_element_type | solution.py:117
  (40 shorter events, 6.1 us)
Async XLA Ops:
  6.5 97.6 %copy-start = (bf16[1280,1280]{1,0:T(8,128)(2,1)S(1)}, bf16[1280,1280]{1,0:T(8,128)(2,1)}, u32[]{:S(2)}) copy-start(bf16[1280,1280]{1,0:T(8,128)(2,1)} %param.22) | copy-start | bytes 9830404
  11.0 15.6 %all-to-all-start = ((s32[16,1,64]{2,1,0:T(1,128)}), s32[16,1,64]{2,1,0:T(1,128)S(1)}, u32[]{:S(2)}, u32[]{:S(2)}) async-start(s32[16,1,64]{2,1,0:T(1,128)} %all_to_all.9), calls=%async_computation.1 | async-start | bytes 16384 | tf_op jit(solution)/shard_map/all_to_all | solution.py:93
  41.3 32.7 %all-to-all-start.1 = ((bf16[16,64,640]{2,1,0:T(8,128)(2,1)}), bf16[16,64,640]{2,1,0:T(8,128)(2,1)}, u32[]{:S(2)}, u32[]{:S(2)}) async-start(bf16[16,64,640]{2,1,0:T(8,128)(2,1)} %dynamic-slice_select_fusion), calls=%async_computation.2 | async-start | bytes 2621440 | tf_op jit(solution)/shard_map/all_to_all | solution.py:97
  45.7 2.3 %copy-start.1 = (bf16[32,2560]{1,0:T(8,128)(2,1)S(1)}, bf16[32,2560]{1,0:T(8,128)(2,1)}, u32[]{:S(2)}) copy-start(bf16[32,2560]{1,0:T(8,128)(2,1)} %param.12) | copy-start | bytes 491524
  45.7 2.5 %copy-start.2 = (f32[2560]{0:T(1024)S(1)}, f32[2560]{0:T(1024)}, u32[]{:S(2)}) copy-start(f32[2560]{0:T(1024)} %param.13) | copy-start | bytes 30724
  45.7 50.5 %all-gather.2.cloned.1.call-start = ((), (), s32[]{:S(2)}) async-start(), calls=%async_computation.4 | async-start | bytes 1966080 | tf_op jit(solution)/shard_map/all_gather | solution.py:99
  50.0 4.9 %copy-start.3 = (s32[32]{0:T(128)S(1)}, s32[32]{0:T(128)}, u32[]{:S(2)}) copy-start(s32[32]{0:T(128)} %param.19) | copy-start | bytes 388
  80.4 27.0 %reduce-scatter.2.cloned.1.call-start = ((), (), s32[]{:S(2)}) async-start(), calls=%async_computation.3 | async-start | bytes 245760 | tf_op jit(solution)/shard_map/reduce_scatter | solution.py:113
Sparse Core Ops, SparseCore 0:
  80.5 10.1 all-gather.1
  93.2 8.5 reduce-scatter.1
where the time goes:
time: 118 us; the launch traced here: 116 us
  local copies, waits for them, and re-layouts  28.2 us (24%)
  matrix products  26.4 us (22%)
  waiting for transfers between devices  20.8 us (18%)
  between operations  13.6 us (12%)
  starting transfers between devices  12.8 us (11%)
  other arithmetic  10.6 us (9%)
  blocking collectives  3.41 us (3%)
    all_to_all x1, waiting for transfers between devices, local(): lax.all_to_all(wanted, 'table', split_axis=0, concat_axis=0, tiled=True)  13.5 us
    gather x1, local copies, waits for them, and re-layouts, local(): jnp.take(table, jnp.maximum(lax.all_to_all(outgoing, 'table', split_axis=...  11.9 us
    all_to_all x1, starting transfers between devices, local(): lax.all_to_all(outgoing, 'table', split_axis=0, concat_axis=0, tiled=True)  8.34 us
    all_to_all x1, waiting for transfers between devices, local(): lax.all_to_all(outgoing, 'table', split_axis=0, concat_axis=0, tiled=True)  7.22 us
    dot_general x1, matrix products, local(): attention = jnp.dot(context, out_weight, preferred_element_type=jnp.float32)  5.05 us
    all_to_all x1, starting transfers between devices, local(): lax.all_to_all(wanted, 'table', split_axis=0, concat_axis=0, tiled=True)  4.38 us
    dot_general x1, matrix products, local(): jnp.einsum('skgh,sckh->skgc', query_heads, key_blocks, preferred_element_...  4.3 us
    dot_general x1, matrix products, local(): jnp.dot(mem_rows, key_proj, preferred_element_type=jnp.float32)  4.29 us
  transfers between devices with their start and end apart: 4, of which 2 were waited for; matrix products, arithmetic and copies ran while one was open for 33% of the time, Pallas kernels for 0%

commit v1 on v0

--- a/solution.py
+++ b/solution.py
@@ -3,12 +3,97 @@
 import jax
 import jax.numpy as jnp
 from jax import lax
+from jax.experimental import pallas as pl
+from jax.experimental.pallas import tpu as pltpu
 from jax.sharding import PartitionSpec as P
 
 HEAD_DIM = 128
 
 
 epsilon = 1e-06
+VMEM_SPEC = pl.BlockSpec(memory_space=pltpu.VMEM)
+
+
+def exchange(x, axis, cid, gather=False):
+    n = lax.axis_size(axis)
+
+    def kernel(x_ref, o_ref, send, recv, here):
+        me = lax.axis_index(axis)
+        peers = [lax.rem(me + k, n) for k in range(1, n)]
+        barrier = pltpu.get_barrier_semaphore()
+        for peer in peers:
+            pl.semaphore_signal(barrier, inc=1, device_id={axis: peer})
+        pl.semaphore_wait(barrier, n - 1)
+        copies = []
+        for k, peer in enumerate(peers):
+            copy = pltpu.make_async_remote_copy(
+                src_ref=x_ref if gather else x_ref.at[peer],
+                dst_ref=o_ref.at[me],
+                send_sem=send.at[k],
+                recv_sem=recv.at[k],
+                device_id={axis: peer},
+            )
+            copy.start()
+            copies.append(copy)
+        own = pltpu.make_async_copy(x_ref if gather else x_ref.at[me], o_ref.at[me], here)
+        own.start()
+        own.wait()
+        for copy in copies:
+            copy.wait()
+
+    shape = (n,) + x.shape if gather else x.shape
+    return pl.pallas_call(
+        kernel,
+        out_shape=jax.ShapeDtypeStruct(shape, x.dtype),
+        in_specs=[VMEM_SPEC],
+        out_specs=VMEM_SPEC,
+        scratch_shapes=[
+            pltpu.SemaphoreType.DMA((n - 1,)),
+            pltpu.SemaphoreType.DMA((n - 1,)),
+            pltpu.SemaphoreType.DMA,
+        ],
+        compiler_params=pltpu.CompilerParams(collective_id=cid, has_side_effects=True),
+    )(x)
+
+
+def pick_rows(ids, table, column, width):
+    count = ids.shape[0]
+    rows = table.shape[0]
+    chunk = math.gcd(rows, 1024)
+    steps = rows // chunk
+
+    def kernel(column_ref, ids_ref, table_ref, o_ref, acc):
+        step = pl.program_id(0)
+        lanes = lax.broadcasted_iota(jnp.int32, (count, chunk), 1) + step * chunk
+        hot = jnp.where(ids_ref[...] == lanes, 1.0, 0.0).astype(jnp.bfloat16)
+        part = jnp.dot(hot, table_ref[...], preferred_element_type=jnp.float32)
+
+        @pl.when(step == 0)
+        def _():
+            acc[...] = part
+
+        @pl.when(step > 0)
+        def _():
+            acc[...] += part
+
+        @pl.when(step == steps - 1)
+        def _():
+            o_ref[...] = acc[...].astype(o_ref.dtype)
+
+    return pl.pallas_call(
+        kernel,
+        grid_spec=pltpu.PrefetchScalarGridSpec(
+            num_scalar_prefetch=1,
+            grid=(steps,),
+            in_specs=[
+                pl.BlockSpec((count, 1), lambda i, c: (0, 0)),
+                pl.BlockSpec((chunk, width), lambda i, c: (i, c[0])),
+            ],
+            out_specs=pl.BlockSpec((count, width), lambda i, c: (0, 0)),
+            scratch_shapes=[pltpu.VMEM((count, width), jnp.float32)],
+        ),
+        out_shape=jax.ShapeDtypeStruct((count, width), table.dtype),
+    )(column.reshape(1), ids.reshape(count, 1), table)
 
 
 def local(
@@ -85,18 +170,24 @@
     earlier = (owner_of[None, :] == owner_of[:, None]) & (positions[None, :] < positions[:, None])
     rank_of = jnp.sum(earlier.astype(jnp.int32), axis=1)
     slot_of = owner_of * capacity + rank_of
-    outgoing = jnp.full((table_count * capacity,), -1, jnp.int32).at[slot_of].set(local_row)
-    outgoing = outgoing.reshape(table_count, capacity)
+    slots = jnp.arange(table_count * capacity, dtype=jnp.int32)
+    outgoing = jnp.max(jnp.where(slots[:, None] == slot_of[None, :], local_row[None, :], -1), axis=1)
+    outgoing = outgoing.reshape(table_count, 1, capacity)
+    outgoing = jnp.pad(outgoing, ((0, 0), (0, 0), (0, -capacity % 128)), constant_values=-1)
     part_width = emb_width // tensor_count
-    wanted = jnp.take(
-        table,
-        jnp.maximum(lax.all_to_all(outgoing, "table", split_axis=0, concat_axis=0, tiled=True), 0),
-        axis=0,
-    )
-    wanted = lax.dynamic_slice_in_dim(wanted, tensor_index * part_width, part_width, 2)
-    replies = lax.all_to_all(wanted, "table", split_axis=0, concat_axis=0, tiled=True)
-    mem_rows = jnp.take(replies.reshape(table_count * capacity, replies.shape[2]), slot_of, axis=0)
-    mem_rows = lax.all_gather(mem_rows, "tensor", axis=1, tiled=True)
+    asked = exchange(outgoing, "table", 0)[:, 0, :capacity].reshape(-1)
+    if part_width % 128 == 0:
+        wanted = pick_rows(asked, table, tensor_index, part_width)
+    else:
+        wanted = pick_rows(asked, table, jnp.zeros_like(tensor_index), emb_width)
+        wanted = lax.dynamic_slice_in_dim(wanted, tensor_index * part_width, part_width, 1)
+    replies = exchange(wanted.reshape(table_count, capacity, part_width), "table", 1)
+    chosen = (slot_of[:, None] == slots[None, :]).astype(jnp.bfloat16)
+    mem_rows = jnp.dot(
+        chosen, replies.reshape(-1, part_width), preferred_element_type=jnp.float32
+    ).astype(jnp.bfloat16)
+    mem_rows = exchange(mem_rows, "tensor", 2, gather=True)
+    mem_rows = jnp.concatenate([mem_rows[j] for j in range(tensor_count)], axis=1)
     lookups = lookup_ids.shape[1]
     mem_key = jnp.dot(mem_rows, key_proj, preferred_element_type=jnp.float32).reshape(
         seq_count, lookups, slice_width
@@ -107,12 +198,13 @@
     normed_slice = lax.dynamic_slice_in_dim(normed, tensor_index * slice_width, slice_width, 1)
     cross_term = jnp.sum(mem_key * normed_slice[:, None, :], axis=-1)
     square_sum = jnp.sum(mem_key * mem_key, axis=-1)
-    cross_term, square_sum = lax.psum((cross_term, square_sum), "tensor")
+    both = exchange(jnp.stack([cross_term, square_sum]), "tensor", 3, gather=True)
+    cross_term, square_sum = jnp.sum(both, axis=0)
     gating = jax.nn.sigmoid(cross_term * lax.rsqrt(square_sum / width + epsilon) / math.sqrt(width))
     memory = jnp.sum(gating[..., None] * mem_value, axis=1)
-    attention_part = lax.psum_scatter(
-        attention.astype(jnp.bfloat16), "tensor", scatter_dimension=1, tiled=True
-    ).astype(jnp.float32)
+    pieces = attention.astype(jnp.bfloat16).reshape(seq_count, tensor_count, slice_width)
+    pieces = exchange(jnp.swapaxes(pieces, 0, 1), "tensor", 4)
+    attention_part = jnp.sum(pieces.astype(jnp.float32), axis=0)
     residual = lax.dynamic_slice_in_dim(hidden_f32, tensor_index * slice_width, slice_width, 1)
     return (residual + attention_part + memory).astype(jnp.bfloat16)
 

time: 118 us -> 114 us (0.966)
  the two profiles are of different devices: /device:TPU:0 before, /device:TPU:15 now
where the time goes in v1:
time: 114 us; the launch traced here: 113 us
  Pallas kernels  66 us (58%)
  matrix products  28.8 us (25%)
  local copies, waits for them, and re-layouts  11.5 us (10%)
  other arithmetic  6.66 us (6%)
    pallas_call x5, Pallas kernels, exchange(): pl.pallas_call(kernel, out_shape=jax.ShapeDtypeStruct(shape, x.dtype), in...  55 us
    pallas_call x1, Pallas kernels, pick_rows(): pl.pallas_call(kernel, grid_spec=pltpu.PrefetchScalarGridSpec(num_scalar_...  11 us
    dot_general x1, matrix products, local(): jnp.dot(mem_rows, key_proj, preferred_element_type=jnp.float32)  4.35 us
    dot_general x1, matrix products, local(): jnp.dot(attn_in, q_weight, preferred_element_type=jnp.float32)  4.15 us
    dot_general x1, matrix products, local(): attention = jnp.dot(context, out_weight, preferred_element_type=jnp.float32)  4.07 us
    dot_general x1, matrix products, local(): jnp.dot(mem_rows, value_proj, preferred_element_type=jnp.float32)  4.01 us
    dot_general x1, matrix products, local(): jnp.einsum('skgc,sckh->skgh', weights_bf, value_blocks, preferred_element...  3.75 us
    dot_general x1, matrix products, local(): jnp.einsum('skgh,sckh->skgc', query_heads, key_blocks, preferred_element_...  3.56 us

profile of v1, /device:TPU:15, one launch (start us, length us, event | category | flops | bytes accessed | tf_op | source)
XLA Modules:
  0.0 113.2 jit_solution(9557764830572876492)
XLA Ops:
  0.0 0.9 copy.23
  2.3 7.9 %shard_map.119 = s32[16,1,128]{2,1,0:T(1,128)} custom-call(s32[16,1,128]{2,1,0:T(1,128)} %pad.4.x_ref), custom_call_target="tpu_custom_call" | custom-call | tf_op jit(solution)/shard_map/pallas_call | solution.py:45
  10.9 1.3 %reshape_reshape_squeeze.4.ids_ref = s32[1024,1]{1,0:T(8,128)} reshape(s32[16,64]{1,0:T(8,128)S(1)} %slice_reduce_fusion) | data formatting | bytes 8192 | tf_op jit(solution)/shard_map/reshape;reshape;squeeze | solution.py:96
  12.2 11.0 %shard_map.120 = bf16[1024,640]{1,0:T(8,128)(2,1)} custom-call(s32[1]{0:T(128)} %bitcast.3.column_ref, s32[1024,1]{1,0:T(8,128)} %reshape_reshape_squeeze.4.ids_ref, bf16[4096,1280]{1,0:T(8,128)(2,1)} %table_ref.1), custom_call_target="tpu_custom_call" | custom-call | tf_op jit(solution)/shard_map/pallas_call | solution.py:83
  23.2 37.2 %shard_map.121 = bf16[16,64,640]{2,1,0:T(8,128)(2,1)} custom-call(bf16[16,64,640]{2,1,0:T(8,128)(2,1)} %bitcast.61), custom_call_target="tpu_custom_call" | custom-call | tf_op jit(solution)/shard_map/pallas_call | solution.py:45
  60.4 3.2 %fusion.8.x_ref = bf16[512,640]{1,0:T(8,128)(2,1)} fusion(bf16[1024,640]{1,0:T(8,128)(2,1)} %bitcast.63, s32[512]{0:T(512)S(1)} %multiply_add_fusion), kind=kOutput, calls=%fused_computation.16 | convolution fusion | flops 671940608 | bytes 1968128 | tf_op jit(solution)/shard_map/dot_general | solution.py:186
  63.7 4.4 %shard_map.122 = bf16[2,512,640]{2,1,0:T(8,128)(2,1)} custom-call(bf16[512,640]{1,0:T(8,128)(2,1)} %fusion.8.x_ref), custom_call_target="tpu_custom_call" | custom-call | tf_op jit(solution)/shard_map/pallas_call | solution.py:45
  68.1 2.5 %slice_bitcast_fusion.1 = (bf16[512,640]{1,0:T(8,128)(2,1)}, bf16[512,640]{1,0:T(8,128)(2,1)}) fusion(bf16[2,512,640]{2,1,0:T(8,128)(2,1)} %shard_map.122), kind=kLoop, calls=%fused_computation.30 | loop fusion | bytes 2621440 | tf_op jit(solution)/shard_map/squeeze | solution.py:190
  70.9 4.3 %fusion.6 = (f32[512]{0:T(512)S(1)}, f32[512]{0:T(512)S(1)}) fusion(f32[32,1280]{1,0:T(8,128)S(1)} %constant_dynamic-slice_fusion, bf16[1280,1280]{1,0:T(8,128)(2,1)} %param.21, bf16[512,640]{1,0:T(8,128)(2,1)} %get-tuple-element.10, bf16[512,640]{1,0:T(8,128)(2,1)} %get-tuple-element.9), kind=kOutput, calls=%fused_computation.8 | convolution fusion | flops 1682963456 | bytes 4755456 | tf_op jit(solution)/shard_map/dot_general | solution.py:192
  76.0 2.6 %shard_map.123 = f32[2,2,32,16]{3,2,1,0:T(8,128)} custom-call(f32[2,32,16]{2,1,0:T(8,128)} %pad_maximum_fusion.3.x_ref), custom_call_target="tpu_custom_call" | custom-call | tf_op jit(solution)/shard_map/pallas_call | solution.py:45
  78.7 0.9 reduce_sum.78
  79.6 4.0 %multiply_reduce_fusion = f32[32,1280]{1,0:T(8,128)} fusion(f32[32,16]{1,0:T(8,128)S(1)} %fusion.36, bf16[1280,1280]{1,0:T(8,128)(2,1)S(1)} %copy-done, bf16[512,640]{1,0:T(8,128)(2,1)} %get-tuple-element.10, bf16[512,640]{1,0:T(8,128)(2,1)} %get-tuple-element.9), kind=kOutput, calls=%fused_computation.9 | convolution fusion | flops 1681612800 | bytes 4753408 | tf_op jit(solution)/shard_map/dot_general | solution.py:195
  85.5 4.2 %convolution_convert_fusion.1 = bf16[32,1280]{1,0:T(8,128)(2,1)S(1)} fusion(bf16[2560,1280]{1,0:T(8,128)(2,1)} %param.14, f32[2560]{0:T(1024)} %param.13, f32[32]{0:T(128)} %copy-done.5, bf16[32,2560]{1,0:T(8,128)(2,1)S(1)} %copy-done.1), kind=kOutput, calls=%fused_computation.11 | convolution fusion | flops 210083840 | bytes 6809728 | tf_op jit(solution)/shard_map/dot_general | solution.py:128
  89.7 0.8 reshape.201
  90.5 1.1 fusion.44
  91.6 0.7 iota_compare_fusion.6
  92.3 3.6 %fusion.43 = (f32[32,2,5]{2,1,0:T(2,128)S(1)}, f32[32,2,5,256]{3,2,1,0:T(8,128)S(1)}) fusion(bf16[32,2,5,128]{3,2,1,0:T(8,128)(2,1)} %reshape.201, pred[32,256]{1,0:T(8,128)(4,1)S(1)} %iota_compare_fusion.6, bf16[32,256,256]{2,1,0:T(8,128)(2,1)} %param.17), kind=kOutput, calls=%fused_computation.74 | convolution fusion | flops 21216960 | bytes 4613376 | tf_op jit(solution)/shard_map/skgh,sckh->skgc/dot_general | solution.py:138
  95.9 0.8 copy-done.3
  98.2 3.8 %fusion.18 = bf16[32,2,5,128]{3,2,1,0:T(8,128)(2,1)} fusion(f32[32,2,5,256]{3,2,1,0:T(8,128)} %copy-done.3, f32[32,2,5]{2,1,0:T(2,128)} %get-tuple-element.12, f32[32,2,5]{2,1,0:T(2,128)S(1)} %multiply_maximum_fusion, f32[32,2,128]{2,1,0:T(2,128)} %reshape.213, f32[32,2,5]{2,1,0:T(2,128)S(1)} %get-tuple-element.11, bf16[32,256,256]{2,1,0:T(8,128)(2,1)} %param.18), kind=kOutput, calls=%fused_computation.21 | convolution fusion | flops 21340160 | bytes 4640512 | tf_op jit(solution)/shard_map/skgc,sckh->skgh/dot_general | solution.py:153
  102.0 1.0 convert_element_type.63
  103.0 4.1 %convolution_convert_fusion = bf16[32,2560]{1,0:T(8,128)(2,1)S(1)} fusion(bf16[32,1280]{1,0:T(8,128)(2,1)S(1)} %convert_element_type.63, bf16[1280,2560]{1,0:T(8,128)(2,1)} %param.16), kind=kOutput, calls=%fused_computation.6 | convolution fusion | flops 209797120 | bytes 6799360 | tf_op jit(solution)/shard_map/dot_general | solution.py:161
  107.7 2.9 %shard_map.118 = bf16[2,32,1280]{2,1,0:T(8,128)(2,1)} custom-call(bf16[2,32,1280]{2,1,0:T(8,128)(2,1)} %bitcast.65), custom_call_target="tpu_custom_call" | custom-call | tf_op jit(solution)/shard_map/pallas_call | solution.py:45
  110.6 1.0 convert_reduce_fusion.1
  111.6 1.6 %add_convert_fusion = bf16[32,1280]{1,0:T(8,128)(2,1)} fusion(f32[32,1280]{1,0:T(8,128)} %multiply_reduce_fusion, f32[32,1280]{1,0:T(8,128)S(1)} %convert_reduce_fusion.1, f32[32,2560]{1,0:T(8,128)S(1)} %convert_element_type.53, s32[]{:T(128)S(6)} %select_n.34), kind=kLoop, calls=%fused_computation.40 | loop fusion | flops 122880 | bytes 573444 | tf_op jit(solution)/shard_map/convert_element_type | solution.py:209
  (37 shorter events, 7.4 us)
Async XLA Ops:
  0.0 79.6 %copy-start = (bf16[1280,1280]{1,0:T(8,128)(2,1)S(1)}, bf16[1280,1280]{1,0:T(8,128)(2,1)}, u32[]{:S(2)}) copy-start(bf16[1280,1280]{1,0:T(8,128)(2,1)} %param.22) | copy-start | bytes 9830404
  63.7 6.9 %copy-start.1 = (bf16[32,2560]{1,0:T(8,128)(2,1)S(1)}, bf16[32,2560]{1,0:T(8,128)(2,1)}, u32[]{:S(2)}) copy-start(bf16[32,2560]{1,0:T(8,128)(2,1)} %param.12) | copy-start | bytes 491524
  70.8 13.3 %copy-start.5 = (f32[32]{0:T(128)}, f32[32]{0:T(128)S(1)}, u32[]{:S(2)}) copy-start(f32[32]{0:T(128)S(1)} %add_rsqrt_fusion) | copy-start | bytes 388
  79.6 4.0 %copy-start.2 = (bf16[2560,2,256]{2,1,0:T(2,128)(2,1)S(1)}, bf16[2560,2,256]{2,1,0:T(2,128)(2,1)}, u32[]{:S(2)}) copy-start(bf16[2560,2,256]{2,1,0:T(2,128)(2,1)} %param.15) | copy-start | bytes 7864324
  83.6 0.7 copy-start.4
  95.9 0.8 copy-start.3

commit v2 on v1

--- a/solution.py
+++ b/solution.py
@@ -96,6 +96,270 @@
     )(column.reshape(1), ids.reshape(count, 1), table)
 
 
+def greet(axis, peers):
+    barrier = pltpu.get_barrier_semaphore()
+    for peer in peers:
+        pl.semaphore_signal(barrier, inc=1, device_id={axis: peer})
+    pl.semaphore_wait(barrier, len(peers))
+
+
+def attend_and_fetch(hidden, gain, qw, kvw, ow, keys, values, lengths, wanted, slot_of):
+    n = lax.axis_size("table")
+    pieces = lax.axis_size("tensor")
+    seqs, width = hidden.shape
+    ctx = keys.shape[1]
+    kvw_cols = kvw.shape[1] // 2
+    q_cols = qw.shape[1]
+    kv_heads = kvw_cols // HEAD_DIM
+    heads = q_cols // HEAD_DIM
+    group = heads // kv_heads
+    pad = -(-heads // 16) * 16
+    batch = math.gcd(seqs, 4)
+    requests = slot_of.shape[0]
+    cap, part = wanted.shape[1:]
+    out_cols = width // pieces
+    inv_scale = 1.0 / math.sqrt(HEAD_DIM)
+
+    def kernel(
+        hid_ref, gain_ref, qw_hbm, kvw_hbm, ow_hbm, k_hbm, v_hbm, len_ref, want_ref, slot_ref,
+        rows_ref, att_ref,
+        qw_v, kvw_v, ow_v, k_v, v_v, got, qbd, ctxs, nkv, send, recv, sems,
+    ):
+        me = lax.axis_index("table")
+        loads = [
+            pltpu.make_async_copy(src, dst, sems.at[i])
+            for i, (src, dst) in enumerate(
+                [(qw_hbm, qw_v), (kvw_hbm, kvw_v), (k_hbm, k_v), (v_hbm, v_v), (ow_hbm, ow_v)]
+            )
+        ]
+        for load in loads:
+            load.start()
+        peers = [lax.rem(me + k, n) for k in range(1, n)]
+        greet("table", peers)
+        copies = []
+        for k, peer in enumerate(peers):
+            copy = pltpu.make_async_remote_copy(
+                src_ref=want_ref.at[peer],
+                dst_ref=got.at[me],
+                send_sem=send.at[k],
+                recv_sem=recv.at[k],
+                device_id={"table": peer},
+            )
+            copy.start()
+            copies.append(copy)
+        own = pltpu.make_async_copy(want_ref.at[me], got.at[me], sems.at[5])
+        own.start()
+        hid = hid_ref[...].astype(jnp.float32)
+        normed = hid * lax.rsqrt(jnp.mean(hid * hid, axis=1, keepdims=True) + epsilon)
+        attn_in = (normed * gain_ref[...]).astype(jnp.bfloat16)
+        qbd[...] = jnp.zeros_like(qbd)
+        loads[0].wait()
+        query = jnp.dot(attn_in, qw_v[...], preferred_element_type=jnp.float32)
+        query = query.astype(jnp.bfloat16).astype(jnp.float32)
+        for j in range(heads):
+            k = j // group
+            qbd[k, pl.ds(j, seqs, stride=pad), :] = query[:, j * HEAD_DIM : (j + 1) * HEAD_DIM]
+        loads[1].wait()
+        new = jnp.dot(attn_in, kvw_v[...], preferred_element_type=jnp.float32)
+        new = new.astype(jnp.bfloat16).astype(jnp.float32)
+        nkv[0] = new[:, :kvw_cols]
+        nkv[1] = new[:, kvw_cols:]
+        loads[2].wait()
+        loads[3].wait()
+        cols = lax.broadcasted_iota(jnp.int32, (1, ctx), 1)
+
+        def step(b, carry):
+            masked, own_scores = [], []
+            for i in range(batch):
+                s = b * batch + i
+                at = pl.ds(pl.multiple_of(s * pad, pad), pad)
+                q = jnp.concatenate([qbd[k, at, :] for k in range(kv_heads)], axis=1)
+                sc = lax.dot_general(
+                    q.astype(jnp.bfloat16),
+                    k_v[s],
+                    (((1,), (1,)), ((), ())),
+                    preferred_element_type=jnp.float32,
+                )
+                masked.append(jnp.where(cols < len_ref[pl.ds(s, 1), :], sc * inv_scale, -1e30))
+                new_key = nkv[0, pl.ds(s, 1), :]
+                own_scores.append(jnp.sum(q * new_key, axis=1, keepdims=True) * inv_scale)
+            masked = jnp.concatenate(masked, axis=0)
+            own_score = jnp.concatenate(own_scores, axis=0)
+            row_max = jnp.maximum(jnp.max(masked, axis=1, keepdims=True), own_score)
+            weights = jnp.exp(masked - row_max)
+            own_weight = jnp.exp(own_score - row_max)
+            denom = jnp.sum(weights, axis=1, keepdims=True) + own_weight
+            probs = (weights / denom).astype(jnp.bfloat16)
+            own_prob = (own_weight / denom).astype(jnp.bfloat16).astype(jnp.float32)
+            for i in range(batch):
+                s = b * batch + i
+                c = jnp.dot(
+                    probs[i * pad : (i + 1) * pad], v_v[s], preferred_element_type=jnp.float32
+                )
+                c = c + own_prob[i * pad : (i + 1) * pad] * nkv[1, pl.ds(s, 1), :]
+                at = pl.ds(pl.multiple_of(s * pad, pad), pad)
+                for k in range(kv_heads):
+                    ctxs[k, at, :] = c[:, k * HEAD_DIM : (k + 1) * HEAD_DIM]
+            return carry
+
+        lax.fori_loop(0, seqs // batch, step, 0)
+        context = jnp.concatenate(
+            [ctxs[j // group, pl.ds(j, seqs, stride=pad), :] for j in range(heads)], axis=1
+        ).astype(jnp.bfloat16)
+        loads[4].wait()
+        att = jnp.dot(context, ow_v[...], preferred_element_type=jnp.float32)
+        att = att.astype(jnp.bfloat16)
+        for t in range(pieces):
+            att_ref[t] = att[:, t * out_cols : (t + 1) * out_cols]
+        slots = lax.broadcasted_iota(jnp.int32, (requests, n * cap), 1)
+        hot = jnp.where(slot_ref[...] == slots, 1.0, 0.0).astype(jnp.bfloat16)
+        own.wait()
+        for copy in copies:
+            copy.wait()
+        picked = jnp.dot(
+            hot, got[...].reshape(n * cap, part), preferred_element_type=jnp.float32
+        )
+        rows_ref[...] = picked.astype(jnp.bfloat16)
+
+    hbm = pl.BlockSpec(memory_space=pl.ANY)
+    return pl.pallas_call(
+        kernel,
+        out_shape=[
+            jax.ShapeDtypeStruct((requests, part), jnp.bfloat16),
+            jax.ShapeDtypeStruct((pieces, seqs, out_cols), jnp.bfloat16),
+        ],
+        in_specs=[VMEM_SPEC, VMEM_SPEC, hbm, hbm, hbm, hbm, hbm, VMEM_SPEC, VMEM_SPEC, VMEM_SPEC],
+        out_specs=[VMEM_SPEC, VMEM_SPEC],
+        scratch_shapes=[
+            pltpu.VMEM(qw.shape, qw.dtype),
+            pltpu.VMEM(kvw.shape, kvw.dtype),
+            pltpu.VMEM(ow.shape, ow.dtype),
+            pltpu.VMEM(keys.shape, keys.dtype),
+            pltpu.VMEM(values.shape, values.dtype),
+            pltpu.VMEM(wanted.shape, wanted.dtype),
+            pltpu.VMEM((kv_heads, seqs * pad, HEAD_DIM), jnp.float32),
+            pltpu.VMEM((kv_heads, seqs * pad, HEAD_DIM), jnp.float32),
+            pltpu.VMEM((2, seqs, kvw_cols), jnp.float32),
+            pltpu.SemaphoreType.DMA((n - 1,)),
+            pltpu.SemaphoreType.DMA((n - 1,)),
+            pltpu.SemaphoreType.DMA((6,)),
+        ],
+        compiler_params=pltpu.CompilerParams(
+            collective_id=1, has_side_effects=True, vmem_limit_bytes=60 * 1024 * 1024
+        ),
+    )(hidden, gain, qw, kvw, ow, keys, values, lengths, wanted, slot_of)
+
+
+def memory_and_mix(hidden, rows, pieces, key_proj, value_proj):
+    n = lax.axis_size("tensor")
+    seqs, width = hidden.shape
+    requests, part = rows.shape
+    lookups = requests // seqs
+    cols = width // n
+
+    def split(x):
+        high = x.astype(jnp.bfloat16)
+        return high, (x - high.astype(jnp.float32)).astype(jnp.bfloat16)
+
+    def dot(a, b):
+        return jnp.dot(a, b, preferred_element_type=jnp.float32)
+
+    def kernel(
+        hid_ref, rows_ref, att_ref, key_hbm, val_hbm, o_ref,
+        key_v, val_v, rows_in, att_in, stat, stat_in, mem_key, sends, recvs, sems,
+    ):
+        me = lax.axis_index("tensor")
+        load_key = pltpu.make_async_copy(key_hbm, key_v, sems.at[0])
+        load_val = pltpu.make_async_copy(val_hbm, val_v, sems.at[1])
+        load_key.start()
+        load_val.start()
+        peers = [lax.rem(me + k, n) for k in range(1, n)]
+        greet("tensor", peers)
+
+        def start(src, dst, group, k, peer):
+            copy = pltpu.make_async_remote_copy(
+                src_ref=src,
+                dst_ref=dst.at[k],
+                send_sem=sends.at[group, k],
+                recv_sem=recvs.at[group, k],
+                device_id={"tensor": peer},
+            )
+            copy.start()
+            return copy
+
+        row_copies = [start(rows_ref, rows_in, 0, k, p) for k, p in enumerate(peers)]
+        att_copies = [start(att_ref.at[p], att_in, 1, k, p) for k, p in enumerate(peers)]
+        origins = [lax.rem(me + n - k, n) for k in range(n)]
+        held = [rows_ref] + [rows_in.at[k] for k in range(n - 1)]
+
+        def part_of(k):
+            return pl.ds(pl.multiple_of(origins[k] * part, math.gcd(part, 128)), part)
+
+        hid = hid_ref[...].astype(jnp.float32)
+        scale = lax.rsqrt(jnp.mean(hid * hid, axis=1, keepdims=True) + epsilon)
+        mine = pl.ds(pl.multiple_of(me * cols, 128), cols)
+        hid_mine = hid_ref[:, mine].astype(jnp.float32)
+        normed = hid_mine * scale
+        load_key.wait()
+        mem_key[...] = dot(rows_ref[...], key_v[part_of(0), :])
+        for k, copy in enumerate(row_copies):
+            copy.wait()
+            mem_key[...] += dot(rows_in[k], key_v[part_of(k + 1), :])
+        mk = mem_key[...]
+        cross = jnp.sum(mk.reshape(seqs, lookups, cols) * normed[:, None, :], axis=2, keepdims=True)
+        square = jnp.sum(mk * mk, axis=1, keepdims=True)
+        lane = lax.broadcasted_iota(jnp.int32, (requests, 128), 1)
+        both = jnp.where(lane == 0, cross.reshape(requests, 1), square)
+        stat[...] = both.T[:8]
+        stat_copies = [start(stat, stat_in, 2, k, p) for k, p in enumerate(peers)]
+        load_val.wait()
+        for copy in att_copies:
+            copy.wait()
+        total = hid_mine + sum(
+            [att_in[k].astype(jnp.float32) for k in range(n - 1)], att_ref[me].astype(jnp.float32)
+        )
+        sums = stat[...]
+        for k, copy in enumerate(stat_copies):
+            copy.wait()
+            sums = sums + stat_in[k]
+        gate = jax.nn.sigmoid(
+            sums[0:1] * lax.rsqrt(sums[1:2] / width + epsilon) / math.sqrt(width)
+        )
+        which = lax.broadcasted_iota(jnp.int32, (seqs, requests), 0) * lookups
+        place = lax.broadcasted_iota(jnp.int32, (seqs, requests), 1)
+        mask = (place >= which) & (place < which + lookups)
+        high, low = split(jnp.where(mask, gate, 0.0))
+        for k in range(n):
+            r = held[k][...]
+            a, b = split(dot(high, r) + dot(low, r))
+            v = val_v[part_of(k), :]
+            total = total + (dot(a, v) + dot(b, v))
+        o_ref[...] = total.astype(o_ref.dtype)
+
+    hbm = pl.BlockSpec(memory_space=pl.ANY)
+    return pl.pallas_call(
+        kernel,
+        out_shape=jax.ShapeDtypeStruct((seqs, cols), jnp.bfloat16),
+        in_specs=[VMEM_SPEC, VMEM_SPEC, VMEM_SPEC, hbm, hbm],
+        out_specs=VMEM_SPEC,
+        scratch_shapes=[
+            pltpu.VMEM(key_proj.shape, key_proj.dtype),
+            pltpu.VMEM(value_proj.shape, value_proj.dtype),
+            pltpu.VMEM((n - 1,) + rows.shape, rows.dtype),
+            pltpu.VMEM((n - 1, seqs, cols), jnp.bfloat16),
+            pltpu.VMEM((8, requests), jnp.float32),
+            pltpu.VMEM((n - 1, 8, requests), jnp.float32),
+            pltpu.VMEM((requests, cols), jnp.float32),
+            pltpu.SemaphoreType.DMA((3, n - 1)),
+            pltpu.SemaphoreType.DMA((3, n - 1)),
+            pltpu.SemaphoreType.DMA((2,)),
+        ],
+        compiler_params=pltpu.CompilerParams(
+            collective_id=2, has_side_effects=True, vmem_limit_bytes=48 * 1024 * 1024
+        ),
+    )(hidden, rows, pieces, key_proj, value_proj)
+
+
 def local(
     hidden,
     attn_gain,
@@ -113,52 +377,7 @@
     seq_count, width = hidden.shape
     tensor_count = lax.axis_size("tensor")
     tensor_index = lax.axis_index("tensor")
-    slice_width = width // tensor_count
-    hidden_f32 = hidden.astype(jnp.float32)
-    normed = hidden_f32 * lax.rsqrt(
-        jnp.mean(hidden_f32 * hidden_f32, axis=1, keepdims=True) + epsilon
-    )
-    attn_in = (normed * attn_gain).astype(jnp.bfloat16)
-    head_dim = HEAD_DIM
-    ctx_len = key_cache.shape[1]
     kv_width = kv_weight.shape[2]
-    kv_local = kv_width // head_dim
-    group_size = q_weight.shape[1] // kv_width
-    inv_scale = 1.0 / math.sqrt(head_dim)
-    query_proj = jnp.dot(attn_in, q_weight, preferred_element_type=jnp.float32).astype(jnp.bfloat16)
-    new_kv = jnp.dot(
-        attn_in, kv_weight.reshape(width, 2 * kv_width), preferred_element_type=jnp.float32
-    ).astype(jnp.bfloat16)
-    query_heads = query_proj.reshape(seq_count, kv_local, group_size, head_dim)
-    new_key = new_kv[:, :kv_width].reshape(seq_count, kv_local, head_dim)
-    new_value = new_kv[:, kv_width:].reshape(seq_count, kv_local, head_dim)
-    key_blocks = key_cache.reshape(seq_count, ctx_len, kv_local, head_dim)
-    value_blocks = value_cache.reshape(seq_count, ctx_len, kv_local, head_dim)
-    attention_energies = (
-        jnp.einsum("skgh,sckh->skgc", query_heads, key_blocks, preferred_element_type=jnp.float32)
-        * inv_scale
-    )
-    own_score = (
-        jnp.einsum("skgh,skh->skg", query_heads, new_key, preferred_element_type=jnp.float32)
-        * inv_scale
-    )
-    valid_mask = jnp.arange(ctx_len, dtype=jnp.int32)[None, :] < cache_lengths[:, None]
-    masked = jnp.where(valid_mask[:, None, None, :], attention_energies, -1e30)
-    row_max = jnp.maximum(jnp.max(masked, axis=-1), own_score)
-    weights = jnp.exp(masked - row_max[..., None])
-    own_weight = jnp.exp(own_score - row_max)
-    denom_sum = jnp.sum(weights, axis=-1) + own_weight
-    weights_bf = (weights / denom_sum[..., None]).astype(jnp.bfloat16)
-    own_prob = (own_weight / denom_sum).astype(jnp.bfloat16)
-    context = jnp.einsum(
-        "skgc,sckh->skgh", weights_bf, value_blocks, preferred_element_type=jnp.float32
-    )
-    context = (
-        context
-        + own_prob.astype(jnp.float32)[..., None] * new_value.astype(jnp.float32)[:, :, None, :]
-    )
-    context = context.reshape(seq_count, -1).astype(jnp.bfloat16)
-    attention = jnp.dot(context, out_weight, preferred_element_type=jnp.float32)
     rows_dev, emb_width = table.shape
     table_count = lax.axis_size("table")
     flat_ids = lookup_ids.reshape(-1)
@@ -181,32 +400,20 @@
     else:
         wanted = pick_rows(asked, table, jnp.zeros_like(tensor_index), emb_width)
         wanted = lax.dynamic_slice_in_dim(wanted, tensor_index * part_width, part_width, 1)
-    replies = exchange(wanted.reshape(table_count, capacity, part_width), "table", 1)
-    chosen = (slot_of[:, None] == slots[None, :]).astype(jnp.bfloat16)
-    mem_rows = jnp.dot(
-        chosen, replies.reshape(-1, part_width), preferred_element_type=jnp.float32
-    ).astype(jnp.bfloat16)
-    mem_rows = exchange(mem_rows, "tensor", 2, gather=True)
-    mem_rows = jnp.concatenate([mem_rows[j] for j in range(tensor_count)], axis=1)
-    lookups = lookup_ids.shape[1]
-    mem_key = jnp.dot(mem_rows, key_proj, preferred_element_type=jnp.float32).reshape(
-        seq_count, lookups, slice_width
+    lengths = jnp.broadcast_to(cache_lengths[:, None], (seq_count, key_cache.shape[1]))
+    mem_rows, pieces = attend_and_fetch(
+        hidden,
+        attn_gain.reshape(1, width),
+        q_weight,
+        kv_weight.reshape(width, 2 * kv_width),
+        out_weight,
+        key_cache,
+        value_cache,
+        lengths,
+        wanted.reshape(table_count, capacity, part_width),
+        slot_of.reshape(requests, 1),
     )
-    mem_value = jnp.dot(mem_rows, value_proj, preferred_element_type=jnp.float32).reshape(
-        seq_count, lookups, slice_width
-    )
-    normed_slice = lax.dynamic_slice_in_dim(normed, tensor_index * slice_width, slice_width, 1)
-    cross_term = jnp.sum(mem_key * normed_slice[:, None, :], axis=-1)
-    square_sum = jnp.sum(mem_key * mem_key, axis=-1)
-    both = exchange(jnp.stack([cross_term, square_sum]), "tensor", 3, gather=True)
-    cross_term, square_sum = jnp.sum(both, axis=0)
-    gating = jax.nn.sigmoid(cross_term * lax.rsqrt(square_sum / width + epsilon) / math.sqrt(width))
-    memory = jnp.sum(gating[..., None] * mem_value, axis=1)
-    pieces = attention.astype(jnp.bfloat16).reshape(seq_count, tensor_count, slice_width)
-    pieces = exchange(jnp.swapaxes(pieces, 0, 1), "tensor", 4)
-    attention_part = jnp.sum(pieces.astype(jnp.float32), axis=0)
-    residual = lax.dynamic_slice_in_dim(hidden_f32, tensor_index * slice_width, slice_width, 1)
-    return (residual + attention_part + memory).astype(jnp.bfloat16)
+    return memory_and_mix(hidden, mem_rows, pieces, key_proj, value_proj)
 
 
 def solution(mesh):

time: 114 us -> 77.9 us (0.68)
  matrix products: 28.8 us -> 0 us
  other arithmetic: 6.66 us -> 1.5 us
  Pallas kernels: 66 us -> 64.8 us
    pallas_call x5 -> x1, Pallas kernels: 55 us -> 7.85 us  [exchange(): pl.pallas_call(kernel, out_shape=jax.ShapeDtypeStruct(shape, x.dtype), in...]
    pallas_call x0 -> x2, Pallas kernels: none -> 45.8 us  [the longest x1 38.3 us: attend_and_fetch(): pl.pallas_call(kernel, out_shape=[jax.ShapeDtypeStruct((requests, part),...]
    dot_general x9 -> x0, matrix products: 28.8 us -> none  [the longest x1 4.35 us: local(): jnp.dot(mem_rows, key_proj, preferred_element_type=jnp.float32)]
    unnamed x14 -> x13, local copies, waits for them, and re-layouts: 2.39 us -> 5.36 us
    squeeze x1 -> x0, local copies, waits for them, and re-layouts: 2.48 us -> none  [local(): mem_rows[j]]
    convert_element_type x4 -> x0, other arithmetic: 2.29 us -> none  [the longest x1 1.59 us: local(): return (residual + attention_part + memory).astype(jnp.bfloat16)]
    reduce_sum x4 -> x0, other arithmetic: 2.23 us -> none  [the longest x1 0.96 us: local(): attention_part = jnp.sum(pieces.astype(jnp.float32), axis=0)]
    convert_element_type x2 -> x0, local copies, waits for them, and re-layouts: 1.63 us -> none  [the longest x1 1.01 us: local(): context = context.reshape(seq_count, -1).astype(jnp.bfloat16)]
where the time goes in v2:
time: 77.9 us; the launch traced here: 77.5 us
  Pallas kernels  64.8 us (83%)
  local copies, waits for them, and re-layouts  11.1 us (14%)
  other arithmetic  1.5 us (2%)
    pallas_call x1, Pallas kernels, attend_and_fetch(): pl.pallas_call(kernel, out_shape=[jax.ShapeDtypeStruct((requests, part),...  38.3 us
    pallas_call x1, Pallas kernels, pick_rows(): pl.pallas_call(kernel, grid_spec=pltpu.PrefetchScalarGridSpec(num_scalar_...  11.2 us
    pallas_call x1, Pallas kernels, exchange(): pl.pallas_call(kernel, out_shape=jax.ShapeDtypeStruct(shape, x.dtype), in...  7.85 us
    pallas_call x1, Pallas kernels, memory_and_mix(): pl.pallas_call(kernel, out_shape=jax.ShapeDtypeStruct((seqs, cols), jnp.b...  7.53 us
    unnamed x13, local copies, waits for them, and re-layouts  5.36 us

profile of v2, /device:TPU:15, one launch (start us, length us, event | category | flops | bytes accessed | tf_op | source)
XLA Modules:
  0.0 77.5 jit_solution(16762224778815270917)
XLA Ops:
  0.0 1.3 %reshape.166.gain_ref = f32[1,2560]{1,0:T(1,128)} reshape(f32[2560]{0:T(1024)} %param.13) | data formatting | bytes 20480 | tf_op jit(solution)/shard_map/reshape | solution.py:406
  1.3 0.8 copy.30
  2.1 0.1 reshape.169
  2.2 0.3 convert_reduce_fusion
  2.5 0.4 select_reduce_fusion
  2.8 0.1 reshape.170
  2.9 0.6 pad.4.x_ref
  3.5 7.9 %shard_map.118 = s32[16,1,128]{2,1,0:T(1,128)} custom-call(s32[16,1,128]{2,1,0:T(1,128)} %pad.4.x_ref), custom_call_target="tpu_custom_call" | custom-call | tf_op jit(solution)/shard_map/pallas_call | solution.py:45
  11.4 0.7 slice_reduce_fusion
  12.1 1.3 %broadcast_in_dim.10.len_ref = s32[32,256]{1,0:T(8,128)} broadcast(s32[32]{0:T(128)} %param.19), dimensions={0} | broadcast | bytes 32896 | tf_op jit(solution)/shard_map/broadcast_in_dim | solution.py:403
  13.4 0.2 reshape.173
  13.6 0.1 copy.38
  13.7 0.9 %fusion.3.slot_ref = s32[512,1]{1,0:T(8,128)} fusion(s32[512,1]{1,0:T(8,128)S(1)} %copy.38, s32[512,1]{1,0:T(8,128)S(1)} %reshape.173), kind=kLoop, calls=%fused_computation.11 | loop fusion | flops 8704 | bytes 6144 | tf_op jit(solution)/shard_map/add | solution.py:391
  14.6 1.3 %reshape_reshape_squeeze.4.ids_ref = s32[1024,1]{1,0:T(8,128)} reshape(s32[16,64]{1,0:T(8,128)S(1)} %slice_reduce_fusion) | data formatting | bytes 8192 | tf_op jit(solution)/shard_map/reshape;reshape;squeeze | solution.py:96
  15.9 11.2 %shard_map.119 = bf16[1024,640]{1,0:T(8,128)(2,1)} custom-call(s32[1]{0:T(128)} %bitcast.column_ref, s32[1024,1]{1,0:T(8,128)} %reshape_reshape_squeeze.4.ids_ref, bf16[4096,1280]{1,0:T(8,128)(2,1)} %table_ref.1), custom_call_target="tpu_custom_call" | custom-call | tf_op jit(solution)/shard_map/pallas_call | solution.py:83
  27.0 0.0 copy-done.4
  27.0 1.9 %copy.39 = bf16[320,8,2,256]{3,1,2,0:T(8,128)(2,1)} copy(bf16[320,8,2,256]{3,2,1,0:T(2,128)(2,1)S(1)} %bitcast.7) | data formatting | bytes 5242880
  29.0 38.3 %shard_map.120 = (bf16[512,640]{1,0:T(8,128)(2,1)}, bf16[2,32,1280]{2,1,0:T(8,128)(2,1)}) custom-call(bf16[32,2560]{1,0:T(8,128)(2,1)} %hid_ref.3, f32[1,2560]{1,0:T(1,128)} %reshape.166.gain_ref, bf16[2560,1280]{1,0:T(8,128)(2,1)} %qw_hbm.1, bf16[2560,512]{1,0:T(8,128)(2,1)} %bitcast.5, bf16[1280,2560]{1,0:T(8,128)(2,1)} %ow_hbm.1, ...), custom_call_target="tpu_custom_call" | custom-call | tf_op jit(solution)/shard_map/pallas_call | solution.py:225
  67.3 0.0 copy-done
  67.3 0.0 copy-done.2
  67.3 1.1 %copy-done.1 = bf16[512,640]{1,0:T(8,128)(2,1)S(1)} copy-done((bf16[512,640]{1,0:T(8,128)(2,1)S(1)}, bf16[512,640]{1,0:T(8,128)(2,1)}, u32[]{:S(2)}) %copy-start.1) | copy-done | bytes 655384
  68.4 0.9 %copy-done.3 = bf16[2,32,1280]{2,1,0:T(8,128)(2,1)S(1)} copy-done((bf16[2,32,1280]{2,1,0:T(8,128)(2,1)S(1)}, bf16[2,32,1280]{2,1,0:T(8,128)(2,1)}, u32[]{:S(2)}) %copy-start.3) | copy-done | bytes 163864
  69.3 7.5 %shard_map.121 = bf16[32,1280]{1,0:T(8,128)(2,1)S(1)} custom-call(bf16[32,2560]{1,0:T(8,128)(2,1)S(1)} %copy-done.2, bf16[512,640]{1,0:T(8,128)(2,1)S(1)} %copy-done.1, bf16[2,32,1280]{2,1,0:T(8,128)(2,1)S(1)} %copy-done.3, bf16[1280,1280]{1,0:T(8,128)(2,1)S(1)} %copy-done, bf16[1280,1280]{1,0:T(8,128)(2,1)} %val_hbm.1), custom_call_target="tpu_custom_call" | custom-call | tf_op jit(solution)/shard_map/pallas_call | solution.py:340
  76.8 0.6 copy.41
  (7 shorter events, 0.0 us)
Async XLA Ops:
  15.9 11.2 %copy-start.4 = (bf16[2560,2,256]{2,1,0:T(2,128)(2,1)S(1)}, bf16[2560,2,256]{2,1,0:T(2,128)(2,1)}, u32[]{:S(2)}) copy-start(bf16[2560,2,256]{2,1,0:T(2,128)(2,1)} %param.15) | copy-start | bytes 7864324
  29.0 38.3 %copy-start = (bf16[1280,1280]{1,0:T(8,128)(2,1)S(1)}, bf16[1280,1280]{1,0:T(8,128)(2,1)}, u32[]{:S(2)}) copy-start(bf16[1280,1280]{1,0:T(8,128)(2,1)} %key_hbm.1) | copy-start | bytes 9830404
  29.0 38.3 %copy-start.2 = (bf16[32,2560]{1,0:T(8,128)(2,1)S(1)}, bf16[32,2560]{1,0:T(8,128)(2,1)}, u32[]{:S(2)}) copy-start(bf16[32,2560]{1,0:T(8,128)(2,1)} %hid_ref.3) | copy-start | bytes 491524
  67.3 1.1 %copy-start.1 = (bf16[512,640]{1,0:T(8,128)(2,1)S(1)}, bf16[512,640]{1,0:T(8,128)(2,1)}, u32[]{:S(2)}) copy-start(bf16[512,640]{1,0:T(8,128)(2,1)} %get-tuple-element.7.rows_ref) | copy-start | bytes 1966084
  68.4 0.9 %copy-start.3 = (bf16[2,32,1280]{2,1,0:T(8,128)(2,1)S(1)}, bf16[2,32,1280]{2,1,0:T(8,128)(2,1)}, u32[]{:S(2)}) copy-start(bf16[2,32,1280]{2,1,0:T(8,128)(2,1)} %get-tuple-element.8.att_ref) | copy-start | bytes 491524

commit v3 on v2

--- a/solution.py
+++ b/solution.py
@@ -14,88 +14,6 @@
 VMEM_SPEC = pl.BlockSpec(memory_space=pltpu.VMEM)
 
 
-def exchange(x, axis, cid, gather=False):
-    n = lax.axis_size(axis)
-
-    def kernel(x_ref, o_ref, send, recv, here):
-        me = lax.axis_index(axis)
-        peers = [lax.rem(me + k, n) for k in range(1, n)]
-        barrier = pltpu.get_barrier_semaphore()
-        for peer in peers:
-            pl.semaphore_signal(barrier, inc=1, device_id={axis: peer})
-        pl.semaphore_wait(barrier, n - 1)
-        copies = []
-        for k, peer in enumerate(peers):
-            copy = pltpu.make_async_remote_copy(
-                src_ref=x_ref if gather else x_ref.at[peer],
-                dst_ref=o_ref.at[me],
-                send_sem=send.at[k],
-                recv_sem=recv.at[k],
-                device_id={axis: peer},
-            )
-            copy.start()
-            copies.append(copy)
-        own = pltpu.make_async_copy(x_ref if gather else x_ref.at[me], o_ref.at[me], here)
-        own.start()
-        own.wait()
-        for copy in copies:
-            copy.wait()
-
-    shape = (n,) + x.shape if gather else x.shape
-    return pl.pallas_call(
-        kernel,
-        out_shape=jax.ShapeDtypeStruct(shape, x.dtype),
-        in_specs=[VMEM_SPEC],
-        out_specs=VMEM_SPEC,
-        scratch_shapes=[
-            pltpu.SemaphoreType.DMA((n - 1,)),
-            pltpu.SemaphoreType.DMA((n - 1,)),
-            pltpu.SemaphoreType.DMA,
-        ],
-        compiler_params=pltpu.CompilerParams(collective_id=cid, has_side_effects=True),
-    )(x)
-
-
-def pick_rows(ids, table, column, width):
-    count = ids.shape[0]
-    rows = table.shape[0]
-    chunk = math.gcd(rows, 1024)
-    steps = rows // chunk
-
-    def kernel(column_ref, ids_ref, table_ref, o_ref, acc):
-        step = pl.program_id(0)
-        lanes = lax.broadcasted_iota(jnp.int32, (count, chunk), 1) + step * chunk
-        hot = jnp.where(ids_ref[...] == lanes, 1.0, 0.0).astype(jnp.bfloat16)
-        part = jnp.dot(hot, table_ref[...], preferred_element_type=jnp.float32)
-
-        @pl.when(step == 0)
-        def _():
-            acc[...] = part
-
-        @pl.when(step > 0)
-        def _():
-            acc[...] += part
-
-        @pl.when(step == steps - 1)
-        def _():
-            o_ref[...] = acc[...].astype(o_ref.dtype)
-
-    return pl.pallas_call(
-        kernel,
-        grid_spec=pltpu.PrefetchScalarGridSpec(
-            num_scalar_prefetch=1,
-            grid=(steps,),
-            in_specs=[
-                pl.BlockSpec((count, 1), lambda i, c: (0, 0)),
-                pl.BlockSpec((chunk, width), lambda i, c: (i, c[0])),
-            ],
-            out_specs=pl.BlockSpec((count, width), lambda i, c: (0, 0)),
-            scratch_shapes=[pltpu.VMEM((count, width), jnp.float32)],
-        ),
-        out_shape=jax.ShapeDtypeStruct((count, width), table.dtype),
-    )(column.reshape(1), ids.reshape(count, 1), table)
-
-
 def greet(axis, peers):
     barrier = pltpu.get_barrier_semaphore()
     for peer in peers:
@@ -103,7 +21,7 @@
     pl.semaphore_wait(barrier, len(peers))
 
 
-def attend_and_fetch(hidden, gain, qw, kvw, ow, keys, values, lengths, wanted, slot_of):
+def attend_and_fetch(hidden, gain, qw, kvw, ow, keys, values, lengths, table, asks, slot_of, cap):
     n = lax.axis_size("table")
     pieces = lax.axis_size("tensor")
     seqs, width = hidden.shape
@@ -116,39 +34,54 @@
     pad = -(-heads // 16) * 16
     batch = math.gcd(seqs, 4)
     requests = slot_of.shape[0]
-    cap, part = wanted.shape[1:]
+    table_rows, emb = table.shape
+    part = emb // pieces
+    aligned = part % 128 == 0
+    held_cols = part if aligned else emb
+    chunk = math.gcd(table_rows, 1024)
+    owners_at_once = math.gcd(n, max(1, 256 // cap))
     out_cols = width // pieces
     inv_scale = 1.0 / math.sqrt(HEAD_DIM)
 
     def kernel(
-        hid_ref, gain_ref, qw_hbm, kvw_hbm, ow_hbm, k_hbm, v_hbm, len_ref, want_ref, slot_ref,
+        hid_ref, gain_ref, qw_hbm, kvw_hbm, ow_hbm, k_hbm, v_hbm, table_hbm, len_ref, ask_ref, slot_ref,
         rows_ref, att_ref,
-        qw_v, kvw_v, ow_v, k_v, v_v, got, qbd, ctxs, nkv, send, recv, sems,
+        qw_v, kvw_v, ow_v, k_v, v_v, table_v, asked, want, got, qbd, ctxs, nkv,
+        ask_send, ask_recv, send, recv, sems,
     ):
         me = lax.axis_index("table")
+        column = lax.axis_index("tensor")
+        table_src = table_hbm
+        if aligned:
+            table_src = table_hbm.at[:, pl.ds(pl.multiple_of(column * part, 128), part)]
         loads = [
             pltpu.make_async_copy(src, dst, sems.at[i])
             for i, (src, dst) in enumerate(
-                [(qw_hbm, qw_v), (kvw_hbm, kvw_v), (k_hbm, k_v), (v_hbm, v_v), (ow_hbm, ow_v)]
+                [
+                    (qw_hbm, qw_v),
+                    (kvw_hbm, kvw_v),
+                    (table_src, table_v),
+                    (k_hbm, k_v),
+                    (v_hbm, v_v),
+                    (ow_hbm, ow_v),
+                ]
             )
         ]
         for load in loads:
             load.start()
         peers = [lax.rem(me + k, n) for k in range(1, n)]
         greet("table", peers)
-        copies = []
+        ask_copies = []
         for k, peer in enumerate(peers):
             copy = pltpu.make_async_remote_copy(
-                src_ref=want_ref.at[peer],
-                dst_ref=got.at[me],
-                send_sem=send.at[k],
-                recv_sem=recv.at[k],
+                src_ref=ask_ref.at[k + 1],
+                dst_ref=asked.at[k],
+                send_sem=ask_send.at[k],
+                recv_sem=ask_recv.at[k],
                 device_id={"table": peer},
             )
             copy.start()
-            copies.append(copy)
-        own = pltpu.make_async_copy(want_ref.at[me], got.at[me], sems.at[5])
-        own.start()
+            ask_copies.append(copy)
         hid = hid_ref[...].astype(jnp.float32)
         normed = hid * lax.rsqrt(jnp.mean(hid * hid, axis=1, keepdims=True) + epsilon)
         attn_in = (normed * gain_ref[...]).astype(jnp.bfloat16)
@@ -164,8 +97,53 @@
         new = new.astype(jnp.bfloat16).astype(jnp.float32)
         nkv[0] = new[:, :kvw_cols]
         nkv[1] = new[:, kvw_cols:]
+        for copy in ask_copies:
+            copy.wait()
+        lanes = ask_ref.shape[2]
+        ids = [ask_ref[0]] + [asked[k] for k in range(n - 1)]
+        filler = -n % 128
+        if filler:
+            ids.append(jnp.full((filler, lanes), -1, jnp.int32))
+        ids = jnp.concatenate(ids, axis=0).astype(jnp.float32).T.astype(jnp.int32)
         loads[2].wait()
+        copies = []
+        order = list(range(1, n)) + [0]
+        for first in range(0, n, owners_at_once):
+            group_ks = order[first : first + owners_at_once]
+            wanted = jnp.concatenate([ids[:cap, k : k + 1] for k in group_ks], axis=0)
+            picked = None
+            for at in range(0, table_rows, chunk):
+                row = lax.broadcasted_iota(jnp.int32, (len(group_ks) * cap, chunk), 1) + at
+                hot = jnp.where(wanted == row, 1.0, 0.0).astype(jnp.bfloat16)
+                term = jnp.dot(
+                    hot, table_v[at : at + chunk, :], preferred_element_type=jnp.float32
+                )
+                picked = term if picked is None else picked + term
+            if not aligned:
+                mine = picked[:, :part]
+                for j in range(1, pieces):
+                    mine = jnp.where(column == j, picked[:, j * part : (j + 1) * part], mine)
+                picked = mine
+            picked = picked.astype(jnp.bfloat16)
+            for i, k in enumerate(group_ks):
+                block = picked[i * cap : (i + 1) * cap]
+                if k == 0:
+                    got[0] = block
+                    continue
+                want[k - 1] = block
+            for k in group_ks:
+                if k > 0:
+                    copy = pltpu.make_async_remote_copy(
+                        src_ref=want.at[k - 1],
+                        dst_ref=got.at[k],
+                        send_sem=send.at[k - 1],
+                        recv_sem=recv.at[k - 1],
+                        device_id={"table": lax.rem(me + n - k, n)},
+                    )
+                    copy.start()
+                    copies.append(copy)
         loads[3].wait()
+        loads[4].wait()
         cols = lax.broadcasted_iota(jnp.int32, (1, ctx), 1)
 
         def step(b, carry):
@@ -180,7 +158,7 @@
                     (((1,), (1,)), ((), ())),
                     preferred_element_type=jnp.float32,
                 )
-                masked.append(jnp.where(cols < len_ref[pl.ds(s, 1), :], sc * inv_scale, -1e30))
+                masked.append(jnp.where(cols < len_ref[s], sc * inv_scale, -1e30))
                 new_key = nkv[0, pl.ds(s, 1), :]
                 own_scores.append(jnp.sum(q * new_key, axis=1, keepdims=True) * inv_scale)
             masked = jnp.concatenate(masked, axis=0)
@@ -206,14 +184,13 @@
         context = jnp.concatenate(
             [ctxs[j // group, pl.ds(j, seqs, stride=pad), :] for j in range(heads)], axis=1
         ).astype(jnp.bfloat16)
-        loads[4].wait()
+        loads[5].wait()
         att = jnp.dot(context, ow_v[...], preferred_element_type=jnp.float32)
         att = att.astype(jnp.bfloat16)
         for t in range(pieces):
             att_ref[t] = att[:, t * out_cols : (t + 1) * out_cols]
         slots = lax.broadcasted_iota(jnp.int32, (requests, n * cap), 1)
         hot = jnp.where(slot_ref[...] == slots, 1.0, 0.0).astype(jnp.bfloat16)
-        own.wait()
         for copy in copies:
             copy.wait()
         picked = jnp.dot(
@@ -228,7 +205,9 @@
             jax.ShapeDtypeStruct((requests, part), jnp.bfloat16),
             jax.ShapeDtypeStruct((pieces, seqs, out_cols), jnp.bfloat16),
         ],
-        in_specs=[VMEM_SPEC, VMEM_SPEC, hbm, hbm, hbm, hbm, hbm, VMEM_SPEC, VMEM_SPEC, VMEM_SPEC],
+        in_specs=[VMEM_SPEC, VMEM_SPEC]
+        + [hbm] * 6
+        + [pl.BlockSpec(memory_space=pltpu.SMEM), VMEM_SPEC, VMEM_SPEC],
         out_specs=[VMEM_SPEC, VMEM_SPEC],
         scratch_shapes=[
             pltpu.VMEM(qw.shape, qw.dtype),
@@ -236,18 +215,23 @@
             pltpu.VMEM(ow.shape, ow.dtype),
             pltpu.VMEM(keys.shape, keys.dtype),
             pltpu.VMEM(values.shape, values.dtype),
-            pltpu.VMEM(wanted.shape, wanted.dtype),
+            pltpu.VMEM((table_rows, held_cols), table.dtype),
+            pltpu.VMEM((n - 1,) + asks.shape[1:], asks.dtype),
+            pltpu.VMEM((n - 1, cap, part), table.dtype),
+            pltpu.VMEM((n, cap, part), table.dtype),
             pltpu.VMEM((kv_heads, seqs * pad, HEAD_DIM), jnp.float32),
             pltpu.VMEM((kv_heads, seqs * pad, HEAD_DIM), jnp.float32),
             pltpu.VMEM((2, seqs, kvw_cols), jnp.float32),
             pltpu.SemaphoreType.DMA((n - 1,)),
             pltpu.SemaphoreType.DMA((n - 1,)),
+            pltpu.SemaphoreType.DMA((n - 1,)),
+            pltpu.SemaphoreType.DMA((n - 1,)),
             pltpu.SemaphoreType.DMA((6,)),
         ],
         compiler_params=pltpu.CompilerParams(
-            collective_id=1, has_side_effects=True, vmem_limit_bytes=60 * 1024 * 1024
+            collective_id=1, has_side_effects=True, vmem_limit_bytes=62 * 1024 * 1024
         ),
-    )(hidden, gain, qw, kvw, ow, keys, values, lengths, wanted, slot_of)
+    )(hidden, gain, qw, kvw, ow, keys, values, table, lengths, asks, slot_of)
 
 
 def memory_and_mix(hidden, rows, pieces, key_proj, value_proj):
@@ -355,7 +339,7 @@
             pltpu.SemaphoreType.DMA((2,)),
         ],
         compiler_params=pltpu.CompilerParams(
-            collective_id=2, has_side_effects=True, vmem_limit_bytes=48 * 1024 * 1024
+            collective_id=2, has_side_effects=True, vmem_limit_bytes=62 * 1024 * 1024
         ),
     )(hidden, rows, pieces, key_proj, value_proj)
 
@@ -375,10 +359,8 @@
     lookup_ids,
 ):
     seq_count, width = hidden.shape
-    tensor_count = lax.axis_size("tensor")
-    tensor_index = lax.axis_index("tensor")
     kv_width = kv_weight.shape[2]
-    rows_dev, emb_width = table.shape
+    rows_dev = table.shape[0]
     table_count = lax.axis_size("table")
     flat_ids = lookup_ids.reshape(-1)
     requests = flat_ids.shape[0]
@@ -388,19 +370,12 @@
     positions = jnp.arange(requests, dtype=jnp.int32)
     earlier = (owner_of[None, :] == owner_of[:, None]) & (positions[None, :] < positions[:, None])
     rank_of = jnp.sum(earlier.astype(jnp.int32), axis=1)
-    slot_of = owner_of * capacity + rank_of
+    turn = lax.rem(owner_of - lax.axis_index("table") + table_count, table_count)
+    slot_of = turn * capacity + rank_of
     slots = jnp.arange(table_count * capacity, dtype=jnp.int32)
     outgoing = jnp.max(jnp.where(slots[:, None] == slot_of[None, :], local_row[None, :], -1), axis=1)
     outgoing = outgoing.reshape(table_count, 1, capacity)
     outgoing = jnp.pad(outgoing, ((0, 0), (0, 0), (0, -capacity % 128)), constant_values=-1)
-    part_width = emb_width // tensor_count
-    asked = exchange(outgoing, "table", 0)[:, 0, :capacity].reshape(-1)
-    if part_width % 128 == 0:
-        wanted = pick_rows(asked, table, tensor_index, part_width)
-    else:
-        wanted = pick_rows(asked, table, jnp.zeros_like(tensor_index), emb_width)
-        wanted = lax.dynamic_slice_in_dim(wanted, tensor_index * part_width, part_width, 1)
-    lengths = jnp.broadcast_to(cache_lengths[:, None], (seq_count, key_cache.shape[1]))
     mem_rows, pieces = attend_and_fetch(
         hidden,
         attn_gain.reshape(1, width),
@@ -409,9 +384,11 @@
         out_weight,
         key_cache,
         value_cache,
-        lengths,
-        wanted.reshape(table_count, capacity, part_width),
+        cache_lengths,
+        table,
+        outgoing,
         slot_of.reshape(requests, 1),
+        capacity,
     )
     return memory_and_mix(hidden, mem_rows, pieces, key_proj, value_proj)
 

time: 77.9 us -> 69 us (0.89)
  the two profiles are of different devices: /device:TPU:15 before, /device:TPU:0 now
where the time goes in v3:
time: 69 us; the launch traced here: 68.7 us
  Pallas kernels  58.7 us (85%)
  local copies, waits for them, and re-layouts  8.37 us (12%)
  other arithmetic  1.58 us (2%)
    pallas_call x1, Pallas kernels, attend_and_fetch(): pl.pallas_call(kernel, out_shape=[jax.ShapeDtypeStruct((requests, part),...  48.6 us
    pallas_call x1, Pallas kernels, memory_and_mix(): pl.pallas_call(kernel, out_shape=jax.ShapeDtypeStruct((seqs, cols), jnp.b...  10.1 us
    unnamed x3, local copies, waits for them, and re-layouts  5.99 us

profile of v3, /device:TPU:0, one launch (start us, length us, event | category | flops | bytes accessed | tf_op | source)
XLA Modules:
  0.0 68.7 jit_solution(11905794027868595622)
XLA Ops:
  0.0 1.3 %reshape.191.gain_ref = f32[1,2560]{1,0:T(1,128)} reshape(f32[2560]{0:T(1024)} %param.13) | data formatting | bytes 20480 | tf_op jit(solution)/shard_map/reshape | solution.py:381
  1.3 0.8 %copy.28 = s32[32,16]{1,0:T(8,128)S(1)} copy(s32[32,16]{0,1:T(8,128)} %param.23) | data formatting | bytes 4096 | tf_op args[11]
  2.1 0.1 reshape.193
  2.2 0.3 convert_reduce_fusion
  2.5 0.4 select_reduce_fusion
  2.8 0.1 reshape.194
  2.9 0.6 pad.4.ask_ref
  3.5 0.2 reshape.196
  3.7 0.1 copy.35
  3.8 0.9 %fusion.6.slot_ref = s32[512,1]{1,0:T(8,128)} fusion(s32[512,1]{1,0:T(8,128)S(1)} %copy.35, s32[512,1]{1,0:T(8,128)S(1)} %reshape.196, s32[]{:T(128)S(6)} %axis_index.15), kind=kLoop, calls=%fused_computation.16 | loop fusion | flops 12800 | bytes 6148 | tf_op jit(solution)/shard_map/add | solution.py:374
  4.8 3.7 %copy.36 = bf16[320,8,2,256]{3,1,2,0:T(8,128)(2,1)} copy(bf16[320,8,2,256]{3,2,1,0:T(2,128)(2,1)} %bitcast.4) | data formatting | bytes 5242880
  8.5 48.6 %shard_map.118 = (bf16[512,640]{1,0:T(8,128)(2,1)}, bf16[2,32,1280]{2,1,0:T(8,128)(2,1)}) custom-call(bf16[32,2560]{1,0:T(8,128)(2,1)} %hid_ref.3, f32[1,2560]{1,0:T(1,128)} %reshape.191.gain_ref, bf16[2560,1280]{1,0:T(8,128)(2,1)} %qw_hbm.1, bf16[2560,512]{1,0:T(8,128)(2,1)} %bitcast.3, bf16[1280,2560]{1,0:T(8,128)(2,1)} %ow_hbm.1, ...), custom_call_target="tpu_custom_call" | custom-call | tf_op jit(solution)/shard_map/pallas_call | solution.py:202
  57.1 10.1 %shard_map.119 = bf16[32,1280]{1,0:T(8,128)(2,1)} custom-call(bf16[32,2560]{1,0:T(8,128)(2,1)} %hid_ref.3, bf16[512,640]{1,0:T(8,128)(2,1)} %get-tuple-element.7.rows_ref, bf16[2,32,1280]{2,1,0:T(8,128)(2,1)} %get-tuple-element.8.att_ref, bf16[1280,1280]{1,0:T(8,128)(2,1)} %key_hbm.1, bf16[1280,1280]{1,0:T(8,128)(2,1)} %val_hbm.1), custom_call_target="tpu_custom_call" | custom-call | tf_op jit(solution)/shard_map/pallas_call | solution.py:324
  67.2 1.5 %copy.38 = bf16[32,1280]{1,0:T(8,128)(2,1)} copy(bf16[32,1280]{1,0:T(8,128)(2,1)} %shard_map.119) | data formatting | bytes 163840
  (2 shorter events, 0.0 us)

commit v4 on v3

--- a/solution.py
+++ b/solution.py
@@ -67,8 +67,7 @@
                 ]
             )
         ]
-        for load in loads:
-            load.start()
+        loads[2].start()
         peers = [lax.rem(me + k, n) for k in range(1, n)]
         greet("table", peers)
         ask_copies = []
@@ -82,21 +81,6 @@
             )
             copy.start()
             ask_copies.append(copy)
-        hid = hid_ref[...].astype(jnp.float32)
-        normed = hid * lax.rsqrt(jnp.mean(hid * hid, axis=1, keepdims=True) + epsilon)
-        attn_in = (normed * gain_ref[...]).astype(jnp.bfloat16)
-        qbd[...] = jnp.zeros_like(qbd)
-        loads[0].wait()
-        query = jnp.dot(attn_in, qw_v[...], preferred_element_type=jnp.float32)
-        query = query.astype(jnp.bfloat16).astype(jnp.float32)
-        for j in range(heads):
-            k = j // group
-            qbd[k, pl.ds(j, seqs, stride=pad), :] = query[:, j * HEAD_DIM : (j + 1) * HEAD_DIM]
-        loads[1].wait()
-        new = jnp.dot(attn_in, kvw_v[...], preferred_element_type=jnp.float32)
-        new = new.astype(jnp.bfloat16).astype(jnp.float32)
-        nkv[0] = new[:, :kvw_cols]
-        nkv[1] = new[:, kvw_cols:]
         for copy in ask_copies:
             copy.wait()
         lanes = ask_ref.shape[2]
@@ -106,8 +90,10 @@
             ids.append(jnp.full((filler, lanes), -1, jnp.int32))
         ids = jnp.concatenate(ids, axis=0).astype(jnp.float32).T.astype(jnp.int32)
         loads[2].wait()
+        for i in (0, 1, 3, 4, 5):
+            loads[i].start()
         copies = []
-        order = list(range(1, n)) + [0]
+        order = sorted(range(1, n), key=lambda k: abs(2 * k - n)) + [0]
         for first in range(0, n, owners_at_once):
             group_ks = order[first : first + owners_at_once]
             wanted = jnp.concatenate([ids[:cap, k : k + 1] for k in group_ks], axis=0)
@@ -142,6 +128,21 @@
                     )
                     copy.start()
                     copies.append(copy)
+        hid = hid_ref[...].astype(jnp.float32)
+        normed = hid * lax.rsqrt(jnp.mean(hid * hid, axis=1, keepdims=True) + epsilon)
+        attn_in = (normed * gain_ref[...]).astype(jnp.bfloat16)
+        qbd[...] = jnp.zeros_like(qbd)
+        loads[0].wait()
+        query = jnp.dot(attn_in, qw_v[...], preferred_element_type=jnp.float32)
+        query = query.astype(jnp.bfloat16).astype(jnp.float32)
+        for j in range(heads):
+            k = j // group
+            qbd[k, pl.ds(j, seqs, stride=pad), :] = query[:, j * HEAD_DIM : (j + 1) * HEAD_DIM]
+        loads[1].wait()
+        new = jnp.dot(attn_in, kvw_v[...], preferred_element_type=jnp.float32)
+        new = new.astype(jnp.bfloat16).astype(jnp.float32)
+        nkv[0] = new[:, :kvw_cols]
+        nkv[1] = new[:, kvw_cols:]
         loads[3].wait()
         loads[4].wait()
         cols = lax.broadcasted_iota(jnp.int32, (1, ctx), 1)
@@ -229,7 +230,7 @@
             pltpu.SemaphoreType.DMA((6,)),
         ],
         compiler_params=pltpu.CompilerParams(
-            collective_id=1, has_side_effects=True, vmem_limit_bytes=62 * 1024 * 1024
+            collective_id=1, has_side_effects=True, vmem_limit_bytes=44 * 1024 * 1024
         ),
     )(hidden, gain, qw, kvw, ow, keys, values, table, lengths, asks, slot_of)
 
@@ -339,7 +340,7 @@
             pltpu.SemaphoreType.DMA((2,)),
         ],
         compiler_params=pltpu.CompilerParams(
-            collective_id=2, has_side_effects=True, vmem_limit_bytes=62 * 1024 * 1024
+            collective_id=2, has_side_effects=True, vmem_limit_bytes=40 * 1024 * 1024
         ),
     )(hidden, rows, pieces, key_proj, value_proj)
 

time: 69 us -> 59.3 us (0.86)
  Pallas kernels: 58.7 us -> 52.7 us
  local copies, waits for them, and re-layouts: 8.37 us -> 5.33 us
  other arithmetic: 1.58 us -> 0.87 us
    pallas_call x1, Pallas kernels: 48.6 us -> 44.9 us  [attend_and_fetch(): pl.pallas_call(kernel, out_shape=[jax.ShapeDtypeStruct((requests, part),...]
    pallas_call x1, Pallas kernels: 10.1 us -> 7.81 us  [memory_and_mix(): pl.pallas_call(kernel, out_shape=jax.ShapeDtypeStruct((seqs, cols), jnp.b...]
    unnamed x3 -> x13, local copies, waits for them, and re-layouts: 5.99 us -> 4.15 us
    add x2, other arithmetic: 0.96 us -> 0.26 us  [local(): slot_of = turn * capacity + rank_of]
where the time goes in v4:
time: 59.3 us; the launch traced here: 59 us
  Pallas kernels  52.7 us (89%)
  local copies, waits for them, and re-layouts  5.33 us (9%)
  other arithmetic  0.87 us (1%)
    pallas_call x1, Pallas kernels, attend_and_fetch(): pl.pallas_call(kernel, out_shape=[jax.ShapeDtypeStruct((requests, part),...  44.9 us
    pallas_call x1, Pallas kernels, memory_and_mix(): pl.pallas_call(kernel, out_shape=jax.ShapeDtypeStruct((seqs, cols), jnp.b...  7.81 us
    unnamed x13, local copies, waits for them, and re-layouts  4.15 us

profile of v4, /device:TPU:0, one launch (start us, length us, event | category | flops | bytes accessed | tf_op | source)
XLA Modules:
  0.0 59.0 jit_solution(259450279873950702)
XLA Ops:
  0.0 0.7 %reshape.191.gain_ref = f32[1,2560]{1,0:T(1,128)S(1)} reshape(f32[2560]{0:T(1024)} %param.13) | data formatting | bytes 20480 | tf_op jit(solution)/shard_map/reshape | solution.py:382
  0.7 0.8 %copy.28 = s32[32,16]{1,0:T(8,128)S(1)} copy(s32[32,16]{0,1:T(8,128)} %param.23) | data formatting | bytes 4096 | tf_op args[11]
  1.5 0.1 reshape.193
  1.6 0.3 convert_reduce_fusion
  1.9 0.4 select_reduce_fusion
  2.2 0.1 reshape.194
  2.3 0.0 copy-start.3
  2.3 0.0 copy-start.4
  2.3 0.2 reshape.196
  2.5 0.1 copy.35
  2.6 0.0 copy-start
  2.7 0.2 fusion.6.slot_ref
  2.9 2.4 %copy.36 = bf16[320,8,2,256]{3,1,2,0:T(8,128)(2,1)S(1)} copy(bf16[320,8,2,256]{3,2,1,0:T(2,128)(2,1)} %bitcast.4) | data formatting | bytes 5242880
  5.3 0.0 copy-done.3
  5.3 0.0 copy-done.4
  5.3 0.4 copy-done
  5.6 0.0 copy-start.1
  5.7 0.0 copy-start.2
  5.7 44.9 %shard_map.118 = (bf16[512,640]{1,0:T(8,128)(2,1)S(1)}, bf16[2,32,1280]{2,1,0:T(8,128)(2,1)S(1)}) custom-call(bf16[32,2560]{1,0:T(8,128)(2,1)S(1)} %copy-done.3, f32[1,2560]{1,0:T(1,128)S(1)} %reshape.191.gain_ref, bf16[2560,1280]{1,0:T(8,128)(2,1)} %qw_hbm.1, bf16[2560,512]{1,0:T(8,128)(2,1)S(1)} %bitcast.3, bf16[1280,2560]{1,0:T(8,128)(2,1)} %ow_hbm.1, ...), custom_call_target="tpu_custom_call" | custom-call | tf_op jit(solution)/shard_map/pallas_call | solution.py:203
  50.5 0.0 copy-done.1
  50.5 0.0 copy-done.2
  50.5 7.8 %shard_map.119 = bf16[32,1280]{1,0:T(8,128)(2,1)S(1)} custom-call(bf16[32,2560]{1,0:T(8,128)(2,1)S(1)} %copy-done.3, bf16[512,640]{1,0:T(8,128)(2,1)S(1)} %get-tuple-element.7.rows_ref, bf16[2,32,1280]{2,1,0:T(8,128)(2,1)S(1)} %get-tuple-element.8.att_ref, bf16[1280,1280]{1,0:T(8,128)(2,1)S(1)} %copy-done.1, bf16[1280,1280]{1,0:T(8,128)(2,1)S(1)} %copy-done.2), custom_call_target="tpu_custom_call" | custom-call | tf_op jit(solution)/shard_map/pallas_call | solution.py:325
  58.4 0.6 %copy.38 = bf16[32,1280]{1,0:T(8,128)(2,1)} copy(bf16[32,1280]{1,0:T(8,128)(2,1)S(1)} %shard_map.119) | data formatting | bytes 163840
  (3 shorter events, 0.0 us)
Async XLA Ops:
  2.3 3.0 %copy-start.3 = (bf16[32,2560]{1,0:T(8,128)(2,1)S(1)}, bf16[32,2560]{1,0:T(8,128)(2,1)}, u32[]{:S(2)}) copy-start(bf16[32,2560]{1,0:T(8,128)(2,1)} %hid_ref.3) | copy-start | bytes 491524
  2.3 3.0 %copy-start.4 = (s32[32]{0:T(128)S(1)}, s32[32]{0:T(128)}, u32[]{:S(2)}) copy-start(s32[32]{0:T(128)} %len_ref.1) | copy-start | bytes 388
  2.6 3.0 %copy-start = (bf16[32,256,256]{2,1,0:T(8,128)(2,1)S(1)}, bf16[32,256,256]{2,1,0:T(8,128)(2,1)}, u32[]{:S(2)}) copy-start(bf16[32,256,256]{2,1,0:T(8,128)(2,1)} %k_hbm.1) | copy-start | bytes 12582916
  5.6 44.9 %copy-start.1 = (bf16[1280,1280]{1,0:T(8,128)(2,1)S(1)}, bf16[1280,1280]{1,0:T(8,128)(2,1)}, u32[]{:S(2)}) copy-start(bf16[1280,1280]{1,0:T(8,128)(2,1)} %key_hbm.1) | copy-start | bytes 9830404
  5.7 44.9 %copy-start.2 = (bf16[1280,1280]{1,0:T(8,128)(2,1)S(1)}, bf16[1280,1280]{1,0:T(8,128)(2,1)}, u32[]{:S(2)}) copy-start(bf16[1280,1280]{1,0:T(8,128)(2,1)} %val_hbm.1) | copy-start | bytes 9830404

commit v5 on v4

--- a/solution.py
+++ b/solution.py
@@ -192,11 +192,24 @@
             att_ref[t] = att[:, t * out_cols : (t + 1) * out_cols]
         slots = lax.broadcasted_iota(jnp.int32, (requests, n * cap), 1)
         hot = jnp.where(slot_ref[...] == slots, 1.0, 0.0).astype(jnp.bfloat16)
-        for copy in copies:
-            copy.wait()
-        picked = jnp.dot(
-            hot, got[...].reshape(n * cap, part), preferred_element_type=jnp.float32
-        )
+        early = order[: n - owners_at_once]
+
+        def compact(first, last):
+            return jnp.dot(
+                hot[:, first * cap : last * cap],
+                got[first:last].reshape((last - first) * cap, part),
+                preferred_element_type=jnp.float32,
+            )
+
+        for copy in copies[: len(early)]:
+            copy.wait()
+        low, high = min(early), max(early) + 1
+        picked = compact(low, high)
+        for copy in copies[len(early) :]:
+            copy.wait()
+        picked = picked + compact(0, low)
+        if high < n:
+            picked = picked + compact(high, n)
         rows_ref[...] = picked.astype(jnp.bfloat16)
 
     hbm = pl.BlockSpec(memory_space=pl.ANY)

time: 59.3 us -> 59.5 us (level)
  no operation moved by 1% of the time
where the time goes in v5:
time: 59.5 us; the launch traced here: 59.2 us
  Pallas kernels  52.9 us (89%)
  local copies, waits for them, and re-layouts  5.33 us (9%)
  other arithmetic  0.87 us (1%)
    pallas_call x1, Pallas kernels, attend_and_fetch(): pl.pallas_call(kernel, out_shape=[jax.ShapeDtypeStruct((requests, part),...  45 us
    pallas_call x1, Pallas kernels, memory_and_mix(): pl.pallas_call(kernel, out_shape=jax.ShapeDtypeStruct((seqs, cols), jnp.b...  7.82 us
    unnamed x13, local copies, waits for them, and re-layouts  4.15 us

profile of v5, /device:TPU:0, one launch (start us, length us, event | category | flops | bytes accessed | tf_op | source)
XLA Modules:
  0.0 59.2 jit_solution(13286561940625979712)
XLA Ops:
  0.0 0.7 %reshape.191.gain_ref = f32[1,2560]{1,0:T(1,128)S(1)} reshape(f32[2560]{0:T(1024)} %param.13) | data formatting | bytes 20480 | tf_op jit(solution)/shard_map/reshape | solution.py:395
  0.7 0.8 %copy.28 = s32[32,16]{1,0:T(8,128)S(1)} copy(s32[32,16]{0,1:T(8,128)} %param.23) | data formatting | bytes 4096 | tf_op args[11]
  1.5 0.1 reshape.193
  1.6 0.3 convert_reduce_fusion
  1.9 0.4 select_reduce_fusion
  2.2 0.1 reshape.194
  2.3 0.0 copy-start.3
  2.3 0.0 copy-start.4
  2.3 0.2 reshape.196
  2.5 0.1 copy.35
  2.6 0.0 copy-start
  2.7 0.2 fusion.6.slot_ref
  2.9 2.4 %copy.36 = bf16[320,8,2,256]{3,1,2,0:T(8,128)(2,1)S(1)} copy(bf16[320,8,2,256]{3,2,1,0:T(2,128)(2,1)} %bitcast.4) | data formatting | bytes 5242880
  5.3 0.0 copy-done.3
  5.3 0.0 copy-done.4
  5.3 0.4 copy-done
  5.6 0.0 copy-start.1
  5.7 0.0 copy-start.2
  5.7 45.0 %shard_map.118 = (bf16[512,640]{1,0:T(8,128)(2,1)S(1)}, bf16[2,32,1280]{2,1,0:T(8,128)(2,1)S(1)}) custom-call(bf16[32,2560]{1,0:T(8,128)(2,1)S(1)} %copy-done.3, f32[1,2560]{1,0:T(1,128)S(1)} %reshape.191.gain_ref, bf16[2560,1280]{1,0:T(8,128)(2,1)} %qw_hbm.1, bf16[2560,512]{1,0:T(8,128)(2,1)S(1)} %bitcast.3, bf16[1280,2560]{1,0:T(8,128)(2,1)} %ow_hbm.1, ...), custom_call_target="tpu_custom_call" | custom-call | tf_op jit(solution)/shard_map/pallas_call | solution.py:216
  50.7 0.0 copy-done.1
  50.7 0.0 copy-done.2
  50.7 7.8 %shard_map.119 = bf16[32,1280]{1,0:T(8,128)(2,1)S(1)} custom-call(bf16[32,2560]{1,0:T(8,128)(2,1)S(1)} %copy-done.3, bf16[512,640]{1,0:T(8,128)(2,1)S(1)} %get-tuple-element.7.rows_ref, bf16[2,32,1280]{2,1,0:T(8,128)(2,1)S(1)} %get-tuple-element.8.att_ref, bf16[1280,1280]{1,0:T(8,128)(2,1)S(1)} %copy-done.1, bf16[1280,1280]{1,0:T(8,128)(2,1)S(1)} %copy-done.2), custom_call_target="tpu_custom_call" | custom-call | tf_op jit(solution)/shard_map/pallas_call | solution.py:338
  58.5 0.6 %copy.38 = bf16[32,1280]{1,0:T(8,128)(2,1)} copy(bf16[32,1280]{1,0:T(8,128)(2,1)S(1)} %shard_map.119) | data formatting | bytes 163840
  (3 shorter events, 0.0 us)
Async XLA Ops:
  2.3 3.0 %copy-start.3 = (bf16[32,2560]{1,0:T(8,128)(2,1)S(1)}, bf16[32,2560]{1,0:T(8,128)(2,1)}, u32[]{:S(2)}) copy-start(bf16[32,2560]{1,0:T(8,128)(2,1)} %hid_ref.3) | copy-start | bytes 491524
  2.3 3.0 %copy-start.4 = (s32[32]{0:T(128)S(1)}, s32[32]{0:T(128)}, u32[]{:S(2)}) copy-start(s32[32]{0:T(128)} %len_ref.1) | copy-start | bytes 388
  2.6 3.0 %copy-start = (bf16[32,256,256]{2,1,0:T(8,128)(2,1)S(1)}, bf16[32,256,256]{2,1,0:T(8,128)(2,1)}, u32[]{:S(2)}) copy-start(bf16[32,256,256]{2,1,0:T(8,128)(2,1)} %k_hbm.1) | copy-start | bytes 12582916
  5.6 45.0 %copy-start.1 = (bf16[1280,1280]{1,0:T(8,128)(2,1)S(1)}, bf16[1280,1280]{1,0:T(8,128)(2,1)}, u32[]{:S(2)}) copy-start(bf16[1280,1280]{1,0:T(8,128)(2,1)} %key_hbm.1) | copy-start | bytes 9830404
  5.7 45.1 %copy-start.2 = (bf16[1280,1280]{1,0:T(8,128)(2,1)S(1)}, bf16[1280,1280]{1,0:T(8,128)(2,1)}, u32[]{:S(2)}) copy-start(bf16[1280,1280]{1,0:T(8,128)(2,1)} %val_hbm.1) | copy-start | bytes 9830404
